TPU v7x, 128 devices: a whole 4x4x4 slice. The times are simulated.
128 devices in a mesh: blk: 8 (over x_lo, y), grid: 16 (over x_hi, z, core).
Axes of the slice: x: 4 (x_hi: 2, x_lo: 2; x = x_hi * 2 + x_lo), y: 4, z: 4, core: 2. Of those that a mesh axis runs over, the one named last changes fastest.
Arguments:
- conn: int32 [2048, 9], P(('blk', 'grid')), may hold values from 0 to 2047, as said below
- extract: float32 [9, 9, 2048], P(None, None, ('blk', 'grid')), may hold values from 0.1 to 1
- points: float32 [3, 9, 2048], P(None, None, ('blk', 'grid')), as said below
Outputs:
- factor: float32 [1, 2048, 2, 1024], P(None, 'grid', None, 'blk')
Inputs may be any that keep to these rules, and one draw needn't show every extreme that they name: `conn`: element e = ix 32 + iy of the periodic 64 x 32 grid of elements names the functions ((ix + s) mod 64) * 32 + (iy + t) mod 32 for s, t in 0, 1, 2, each once, in an order that differs from element to element. The 9 points of element e = ix 32 + iy are the 3 x 3 Gauss points of the cell [ix / 64, (ix + 1) / 64] x [iy / 64, (iy + 1) / 64], each coordinate then moved by at most 3.5 / 64; points[2] is positive.
All inputs are finite; a program needn't handle non-finite values.
Results may differ from a plain program's by a relative error of at most 0.0003.
Values sent between devices are 32-bit elements; how exact they have to be, the bound alone decides.
A program may use at most 128 MiB of HBM per device.

v0:
```python
import math

import jax
import jax.numpy as jnp
from jax import lax
from jax.sharding import PartitionSpec as P

M = 2048
EX = 64
EY = 32
QP = 9
TB = 128


kernel_gain = 0.02
mass_shift = 0.05


def spread(array, axis, root):
    mine = lax.axis_index(axis) == root
    return lax.psum(jnp.where(mine, array, jnp.zeros_like(array)), axis)


def bernstein_table():
    spread_root = 0.5 * math.sqrt(0.6)
    gauss_nodes = [0.5 - spread_root, 0.5, 0.5 + spread_root]

    def bern_poly(which, where):
        return [(1.0 - where) ** 2, 2.0 * where * (1.0 - where), where * where][which]

    table_rows = []
    for i in range(3):
        for j in range(3):
            table_row = []
            for a in range(3):
                for b in range(3):
                    table_row.append(bern_poly(a, gauss_nodes[i]) * bern_poly(b, gauss_nodes[j]))
            table_rows.append(table_row)
    return jnp.asarray(table_rows, jnp.float32)


def torus_square(first_x, first_y, second_x, second_y):
    height = EY / EX
    gap_x = jnp.abs(first_x - second_x)
    gap_x = jnp.minimum(gap_x, jnp.abs(1.0 - gap_x))
    gap_y = jnp.abs(first_y - second_y)
    gap_y = jnp.minimum(gap_y, jnp.abs(height - gap_y))
    return gap_x * gap_x + gap_y * gap_y


def kernel_rows(test_x, test_y, trial_x, trial_y, trial_w):
    distance = torus_square(test_x[:, None], test_y[:, None], trial_x[None, :], trial_y[None, :])
    return kernel_gain * trial_w[None, :] * (1.0 + distance * (EX * EX / 4.0)) ** (-1.75)


def local_values(extract_cube):
    return jnp.einsum(
        "kb,abn->nka", bernstein_table(), extract_cube, precision=lax.Precision.HIGHEST
    )


def basis_rows(values, links):
    count = links.shape[0]
    slot = jnp.arange(count * QP, dtype=jnp.int32).reshape(count, QP)
    row_index = jnp.broadcast_to(slot[:, :, None], (count, QP, QP))
    col_index = jnp.broadcast_to(links[:, None, :], (count, QP, QP))
    return jnp.zeros((count * QP, M), jnp.float32).at[row_index, col_index].add(values)


def window_width():
    wide = 128 + 4 * EY
    return wide


def fold_window(potential_wide):
    extra = potential_wide.shape[1] - M
    return potential_wide[:, :M] + jnp.pad(potential_wide[:, M:], ((0, 0), (0, M - extra)))


def tile_target(links, grid_size, tile_rows):
    tile = links // TB
    return tile % grid_size * (tile_rows * TB) + tile // grid_size * TB + links % TB


def add_potential(state, piece, first_element, test_x, test_y):
    points_flat, extract_flat, links_flat = piece
    count = points_flat.shape[1]
    span = math.gcd(count, 128)
    width = window_width()
    window_iota = jnp.arange(width, dtype=jnp.int32)

    def step(index, inner):
        potential_wide, total = inner
        first = index * span
        part_points = lax.dynamic_slice_in_dim(points_flat, first, span, 1).reshape(3, QP, span)
        part_extract = lax.dynamic_slice_in_dim(extract_flat, first, span, 1).reshape(QP, QP, span)
        part_links = lax.dynamic_slice_in_dim(links_flat, first, span, 1).T
        kernel_block = kernel_rows(
            test_x,
            test_y,
            part_points[0].T.reshape(-1),
            part_points[1].T.reshape(-1),
            part_points[2].T.reshape(-1),
        )
        total = total + jnp.sum(kernel_block, axis=1)
        offset = (first_element + first) // EY * EY
        local = (part_links - offset) % M
        ones = (local[:, :, None] == window_iota[None, None, :]).astype(jnp.float32)
        trial_phi = jnp.einsum(
            "eka,eaw->ekw", local_values(part_extract), ones, precision=lax.Precision.HIGHEST
        ).reshape(span * QP, width)
        block = jnp.dot(
            kernel_block,
            trial_phi,
            precision=lax.Precision.HIGHEST,
            preferred_element_type=jnp.float32,
        )
        current = lax.dynamic_slice_in_dim(potential_wide, offset, width, 1)
        potential_wide = lax.dynamic_update_slice_in_dim(potential_wide, current + block, offset, 1)
        return (potential_wide, total)

    return lax.fori_loop(0, count // span, step, state)


def shards(conn, extract, points):
    count = conn.shape[0]
    rows = count * QP
    links_flat = conn.T
    extract_flat = extract.reshape(QP * QP, count)
    points_flat = points.reshape(3 * QP, count)
    own_x = points[0].T.reshape(-1)
    own_y = points[1].T.reshape(-1)
    own_w = points[2].T.reshape(-1)
    own_values = local_values(extract)
    test_phi = basis_rows(own_values, conn)
    width = window_width()
    start_state = (jnp.zeros((rows, M + width), jnp.float32), jnp.zeros((rows,), jnp.float32))
    grid_size = lax.axis_size("grid")
    blk_size = lax.axis_size("blk")
    grid_at = lax.axis_index("grid")
    blk_at = lax.axis_index("blk")
    tile_rows = M // (TB * grid_size)
    tile_cols = M // (TB * blk_size)
    band = tile_cols * TB
    potential_wide, total = add_potential(
        start_state,
        (
            lax.all_gather(points_flat, ("blk", "grid"), axis=1, tiled=True),
            lax.all_gather(extract_flat, ("blk", "grid"), axis=1, tiled=True),
            lax.all_gather(links_flat, ("blk", "grid"), axis=1, tiled=True),
        ),
        jnp.int32(0),
        own_x,
        own_y,
    )
    potential = fold_window(potential_wide)
    share = own_w[:, None] * ((mass_shift + total)[:, None] * test_phi - potential)
    own_contrib = jnp.einsum(
        "eka,ekm->eam", own_values, share.reshape(count, QP, M), precision=lax.Precision.HIGHEST
    )
    split_cols = (
        own_contrib.reshape(rows, tile_cols, blk_size, TB)
        .transpose(2, 0, 1, 3)
        .reshape(blk_size, rows, band)
    )
    targets = tile_target(conn.reshape(-1), grid_size, tile_rows)
    placed = (
        jnp.zeros((blk_size, grid_size * tile_rows * TB, band), jnp.float32)
        .at[:, targets]
        .add(split_cols)
    )
    term = placed.reshape(blk_size * grid_size, -1)
    stiff = lax.psum_scatter(term, ("blk", "grid"), scatter_dimension=0, tiled=True).reshape(
        tile_rows, TB, tile_cols, TB
    )
    column_tiles = stiff[:, :, 0, :]
    mine = spread(column_tiles, "blk", 0)
    panel_tiles = lax.all_gather(mine, "grid", axis=0, tiled=True)
    panel = panel_tiles.reshape(grid_size, tile_rows, TB, TB).transpose(1, 0, 2, 3).reshape(M, TB)
    head = panel[:TB]
    lower = jnp.linalg.cholesky(0.5 * (head + head.T))
    rest = lax.linalg.triangular_solve(
        lower, panel[TB:], left_side=False, lower=True, transpose_a=True
    )
    factor_cols = jnp.concatenate([lower, rest], axis=0)
    row_part = lax.dynamic_index_in_dim(
        factor_cols.reshape(tile_rows, grid_size, TB, TB), grid_at, 1, keepdims=False
    )
    col_part = lax.dynamic_index_in_dim(
        factor_cols.reshape(tile_cols, blk_size, TB, TB), blk_at, 1, keepdims=False
    )
    update = jnp.einsum("xuw,yvw->xuyv", row_part, col_part, precision=lax.Precision.HIGHEST)
    tile_row = (jnp.arange(tile_rows, dtype=jnp.int32) * grid_size + grid_at)[:, None, None, None]
    tile_col = (jnp.arange(tile_cols, dtype=jnp.int32) * blk_size + blk_at)[None, None, :, None]
    whole_row = tile_row * TB + jnp.arange(TB, dtype=jnp.int32)[None, :, None, None]
    whole_col = tile_col * TB + jnp.arange(TB, dtype=jnp.int32)[None, None, None, :]
    trailing = stiff - update
    result = jnp.where(
        tile_col == 0, row_part[:, :, None, :], jnp.where(tile_row == 0, 0.0, trailing)
    )
    return jnp.where(whole_row >= whole_col, result, 0.0)


def solution(mesh):
    in_specs = (
        P(("blk", "grid"), None),
        P(None, None, ("blk", "grid")),
        P(None, None, ("blk", "grid")),
    )
    out_specs = P(None, "grid", None, "blk")
    return jax.shard_map(shards, mesh=mesh, in_specs=in_specs, out_specs=out_specs, check_vma=False)
```

profile of v0, /device:TPU:127, one launch (start us, length us, event | category | flops | bytes accessed | tf_op | source)
XLA Modules:
  0.0 1180.9 jit_solution(11756267952525601225)
XLA Ops:
  13.7 172.6 %all_gather.13 = f32[81,2048]{0,1:T(8,128)S(1)} all-gather(f32[81,16]{0,1:T(8,128)S(1)} %copy.82), channel_id=1, replica_groups=mesh['blk'=8,'grid'=16] {'blk','grid'}, dimensions={1}, use_global_device_ids=true | all-gather | bytes 668736 | tf_op jit(solution)/shard_map/all_gather | solution.py:149
  187.6 185.9 %all_gather.12 = f32[27,2048]{0,1:T(8,128)} all-gather(f32[27,16]{0,1:T(8,128)S(1)} %reshape.418), channel_id=1, replica_groups=mesh['blk'=8,'grid'=16] {'blk','grid'}, dimensions={1}, use_global_device_ids=true | all-gather | bytes 222912 | tf_op jit(solution)/shard_map/all_gather | solution.py:148
  373.5 183.4 %all_gather.14 = s32[9,2048]{0,1:T(8,128)} all-gather(s32[9,16]{0,1:T(8,128)S(1)} %bitcast.107), channel_id=1, replica_groups=mesh['blk'=8,'grid'=16] {'blk','grid'}, dimensions={1}, use_global_device_ids=true | all-gather | bytes 74304 | tf_op jit(solution)/shard_map/all_gather | solution.py:150
  559.0 172.8 %while.20 = (s32[]{:T(128)}, f32[144,2304]{1,0:T(8,128)}, f32[144]{0:T(256)S(1)}, f32[27,2048]{0,1:T(8,128)}, f32[16,9]{1,0:T(8,128)}, /*index=5*/f32[16,9]{1,0:...) while((s32[]{:T(128)}, f32[144,2304]{1,0:T(8,128)}, ...), condition=%wide.wide.region_2.3_spmd.clone.clone, body=%wide.wide.region_0.2_spmd.sunk.clone.clone.sunk | while | flops 548399360 | bytes 5783860 | solution.py:122
  561.4 1.5 fusion.61
  564.8 2.4 convolution_add_fusion.3
  567.2 1.7 dynamic_update_slice.15
  572.3 1.5 fusion.61
  575.7 2.4 convolution_add_fusion.3
  578.1 1.7 dynamic_update_slice.15
  583.1 1.5 fusion.61
  586.5 2.4 convolution_add_fusion.3
  588.9 1.7 dynamic_update_slice.15
  593.9 1.5 fusion.61
  597.3 2.4 convolution_add_fusion.3
  599.7 1.7 dynamic_update_slice.15
  604.7 1.5 fusion.61
  608.1 2.4 convolution_add_fusion.3
  610.5 1.7 dynamic_update_slice.15
  615.5 1.5 fusion.61
  618.9 2.4 convolution_add_fusion.3
  621.3 1.7 dynamic_update_slice.15
  629.7 2.4 convolution_add_fusion.3
  632.1 1.7 dynamic_update_slice.15
  637.1 1.5 fusion.61
  640.5 2.4 convolution_add_fusion.3
  642.9 1.7 dynamic_update_slice.15
  647.9 1.5 fusion.61
  651.3 2.4 convolution_add_fusion.3
  653.7 1.7 dynamic_update_slice.15
  658.7 1.5 fusion.61
  662.1 2.4 convolution_add_fusion.3
  664.5 1.7 dynamic_update_slice.15
  669.5 1.5 fusion.61
  672.9 2.4 convolution_add_fusion.3
  675.3 1.7 dynamic_update_slice.15
  680.3 1.5 fusion.61
  683.7 2.4 convolution_add_fusion.3
  686.1 1.7 dynamic_update_slice.15
  691.1 1.5 fusion.61
  694.5 2.4 convolution_add_fusion.3
  696.9 1.7 dynamic_update_slice.15
  702.0 1.5 fusion.61
  705.4 2.4 convolution_add_fusion.3
  707.8 1.7 dynamic_update_slice.15
  712.8 1.5 fusion.61
  716.2 2.4 convolution_add_fusion.3
  718.6 1.7 dynamic_update_slice.15
  723.5 1.5 fusion.61
  726.9 2.4 convolution_add_fusion.3
  729.3 1.7 dynamic_update_slice.15
  735.9 9.4 scatter_custom_fusion.1
  747.2 1.5 subtract_multiply_fusion
  748.9 3.3 fusion.33
  752.2 1.6 reshape.384
  753.8 6.0 broadcast_in_dim.83
  759.8 16.2 %scatter_fusion = f32[8,2048,256]{2,0,1:T(8,128)} fusion(f32[8,2048,256]{2,0,1:T(8,128)} %broadcast_in_dim.83, s32[144]{0:T(256)S(1)} %bitcast.113, f32[144,8,256]{2,1,0:T(8,128)S(1)} %bitcast.99), kind=kCustom, calls=%fused_computation | custom fusion | flops 294912 | bytes 3539520 | tf_op jit(solution)/shard_map/scatter-add | solution.py:170
  776.0 15.8 %copy.93 = f32[8,2048,256]{2,1,0:T(8,128)} copy(f32[8,2048,256]{2,0,1:T(8,128)} %scatter_fusion) | data formatting | bytes 33554432 | tf_op jit(solution)/shard_map/scatter-add | solution.py:170
  791.8 18.2 %reshape.386 = f32[128,32768]{1,0:T(8,128)} reshape(f32[8,2048,256]{2,1,0:T(8,128)} %copy.93) | data formatting | bytes 33554432 | tf_op jit(solution)/shard_map/reshape | solution.py:172
  810.1 215.9 %all-reduce.7.cloned.1.call-done = f32[128,32768]{1,0:T(8,128)} async-done(((f32[128,32768]{1,0:T(8,128)}), f32[128,32768]{1,0:T(8,128)}) %all-reduce.7.cloned.1.call-update) | async-done | bytes 16777232
  1028.3 67.0 %all-reduce.5.cloned.1.call-done = f32[1,128,128]{2,1,0:T(8,128)} async-done(((f32[1,128,128]{2,1,0:T(8,128)}), f32[1,128,128]{2,1,0:T(8,128)}) %all-reduce.5.cloned.1.call-update) | async-done | bytes 65552 | tf_op jit(solution)/shard_map/psum | solution.py:21
  1095.5 51.9 %all-gather.2.cloned.1.call-done = f32[16,128,128]{2,1,0:T(8,128)} async-done(((f32[1,128,128]{2,1,0:T(8,128)}), f32[16,128,128]{2,1,0:T(8,128)}) %all-gather.2.cloned.1.call-update) | async-done | bytes 1048592 | tf_op jit(solution)/shard_map/all_gather | solution.py:178
  1149.4 11.7 cholesky.18
  1162.4 9.8 custom-call.6
  (281 shorter events, 107.1 us)
Async XLA Ops:
  6.5 1019.5 %all-reduce.7.cloned.1.call-start = ((), (), s32[]{:S(2)}) async-start(), calls=%async_computation.2 | async-start | bytes 33554432
  12.4 175.1 %copy-start.4 = (f32[1,9,16]{1,2,0:T(8,128)}, f32[1,9,16]{1,2,0:T(8,128)S(1)}, u32[]{:S(2)}) copy-start(f32[1,9,16]{1,2,0:T(8,128)S(1)} %copy.103) | copy-start | bytes 1732
  12.6 174.9 %copy-start.5 = (f32[1,9,16]{1,2,0:T(8,128)}, f32[1,9,16]{1,2,0:T(8,128)S(1)}, u32[]{:S(2)}) copy-start(f32[1,9,16]{1,2,0:T(8,128)S(1)} %copy.102) | copy-start | bytes 1732
  186.3 187.3 %copy-start.3 = (s32[16,9]{1,0:T(8,128)S(1)}, s32[16,9]{1,0:T(8,128)}, u32[]{:S(2)}) copy-start(s32[16,9]{1,0:T(8,128)} %param.7) | copy-start | bytes 1732
  187.5 369.5 %copy-start.1 = (f32[9,9,1]{1,0,2:T(8,128)S(1)}, f32[9,9,1]{1,0,2:T(8,128)}, u32[]{:S(2)}) copy-start(f32[9,9,1]{1,0,2:T(8,128)} %constant.314) | copy-start | bytes 976
  187.5 369.5 %copy-start.2 = (f32[9,9,16]{2,1,0:T(8,128)S(1)}, f32[9,9,16]{2,1,0:T(8,128)}, u32[]{:S(2)}) copy-start(f32[9,9,16]{2,1,0:T(8,128)} %param.8) | copy-start | bytes 15556
  559.0 174.9 %copy-start.9 = (s32[2]{0:T(128)S(1)}, s32[2]{0:T(128)}, u32[]{:S(2)}) copy-start(s32[2]{0:T(128)} %constant.303) | copy-start | bytes 28
  559.0 175.1 %copy-start.8 = (s32[2]{0:T(128)S(1)}, s32[2]{0:T(128)}, u32[]{:S(2)}) copy-start(s32[2]{0:T(128)} %constant.306) | copy-start | bytes 28
  745.4 1.2 copy-start.6
  745.4 1.8 copy-start
  752.2 1.6 copy-start.7
  810.1 285.3 %all-reduce.5.cloned.1.call-start = ((), (), s32[]{:S(2)}) async-start(), calls=%async_computation | async-start | bytes 131072 | tf_op jit(solution)/shard_map/psum | solution.py:21
  1028.0 119.4 %all-gather.2.cloned.1.call-start = ((), (), s32[]{:S(2)}) async-start(), calls=%async_computation.1 | async-start | bytes 1114112 | tf_op jit(solution)/shard_map/all_gather | solution.py:178
  1149.2 23.0 %slice-start = ((f32[16,128,128]{2,1,0:T(8,128)}), f32[15,128,128]{2,1,0:T(8,128)S(1)}, s32[]{:S(2)}) async-start(f32[16,128,128]{2,1,0:T(8,128)} %all-gather.2.cloned.1.call-done), calls=%async_computation.3 | async-start | bytes 1966080 | tf_op jit(solution)/shard_map/slice | solution.py:183
Sparse Core Ops, SparseCore 0:
  810.2 215.7 all-reduce.6
  1028.6 66.7 all-reduce.4
  1097.8 49.5 all-gather.1
where the time goes:
time: 1190 us; the launch traced here: 1180 us
  blocking collectives  542 us (46%)
  waiting for transfers between devices  335 us (28%)
  local copies, waits for them, and re-layouts  120 us (10%)
  other arithmetic  98.2 us (8%)
  matrix products  70.7 us (6%)
  between operations  13.4 us (1%)
    unnamed x4, waiting for transfers between devices  216 us
    all_gather x1, blocking collectives, shards(): lax.all_gather(points_flat, ('blk', 'grid'), axis=1, tiled=True)  186 us
    all_gather x1, blocking collectives, shards(): lax.all_gather(links_flat, ('blk', 'grid'), axis=1, tiled=True)  183 us
    all_gather x1, blocking collectives, shards(): lax.all_gather(extract_flat, ('blk', 'grid'), axis=1, tiled=True)  173 us
    psum x1, waiting for transfers between devices, spread(): return lax.psum(jnp.where(mine, array, jnp.zeros_like(array)), axis)  67 us
    all_gather x1, waiting for transfers between devices, shards(): panel_tiles = lax.all_gather(mine, 'grid', axis=0, tiled=True)  51.9 us
    dot_general x16, matrix products, step(): jnp.dot(kernel_block, trial_phi, precision=lax.Precision.HIGHEST, preferr...  38.3 us
    dynamic_update_slice x16, local copies, waits for them, and re-layouts, step(): lax.dynamic_update_slice_in_dim(potential_wide, current + block, offset, 1)  27.4 us
  transfers between devices with their start and end apart: 3, of which 3 were waited for; matrix products, arithmetic and copies ran while one was open for 0% of the time, Pallas kernels for 0%

commit v1 on v0

v1 whole, which is shorter than its diff:
```python
import functools
import math

import jax
import jax.numpy as jnp
import numpy as np
from jax import lax
from jax.experimental import pallas as pl
from jax.experimental.pallas import tpu as pltpu
from jax.sharding import PartitionSpec as P

M = 2048
EX = 64
EY = 32
QP = 9
TB = 128
BLK = 8
GRID = 16
PTS = QP * TB
WIN = 256
AUG = 192

KERNEL_GAIN = 0.02
MASS_SHIFT = 0.05

FX, FY, FW, FV, FC = 0, 9, 18, 27, 108

MESH = pl.DeviceIdType.MESH
VMEM_LIMIT = 48 * 1024 * 1024
EXACT = lax.Precision.HIGHEST


def bernstein_table():
    spread_root = 0.5 * math.sqrt(0.6)
    nodes = [0.5 - spread_root, 0.5, 0.5 + spread_root]
    poly = [[(1.0 - t) ** 2, 2.0 * t * (1.0 - t), t * t] for t in nodes]
    return np.array(
        [
            [poly[i][a] * poly[j][b] for a in range(3) for b in range(3)]
            for i in range(3)
            for j in range(3)
        ],
        np.float32,
    )


def field_map():
    table = np.zeros((TB, TB), np.float32)
    bern = bernstein_table()
    for i in range(FV):
        table[i, i] = 1.0
    for i in range(FC, FC + QP):
        table[i, i] = 1.0
    for k in range(QP):
        for a in range(QP):
            for b in range(QP):
                table[FV + k * QP + a, FV + a * QP + b] = bern[k, b]
    return table


def pair_device(first, second):
    hi, lo = jnp.maximum(first, second), jnp.minimum(first, second)
    same = hi == lo
    low = lo < BLK
    b = jnp.where(same, hi % BLK, jnp.where(low, lo, hi - BLK))
    g = jnp.where(same, hi % BLK, jnp.where(low, hi, lo - BLK))
    return b, g


def here():
    return lax.axis_index("blk"), lax.axis_index("grid")


def own_pair(b, g):
    diag = b == g
    hi = jnp.where(g >= b, g, b + BLK)
    lo = jnp.where(g > b, b, g + BLK)
    return hi, lo, diag


def greet(barrier, b, g):
    pl.semaphore_signal(barrier, inc=1, device_id=(b, g), device_id_type=MESH)


def gather_greetings(barrier, number):
    @pl.when(number > 0)
    def _():
        pl.semaphore_wait(barrier, number)


def differs(b, g, mb, mg):
    return jnp.logical_or(b != mb, g != mg)


def gather_kernel(map_ref, conn_ref, extract_ref, points_ref, out_ref, raw, record, send_sem, recv_sem):
    mb, mg = here()
    hi, lo, diag = own_pair(mb, mg)
    block = 2 * mb + mg // 8
    place = mg % 8
    barrier = pltpu.get_barrier_semaphore()

    def source(n):
        wanted = jnp.where(n // 8 == 0, hi, lo)
        return wanted // 2, (wanted % 2) * 8 + n % 8

    def say(n, carry):
        b, g = source(n)

        @pl.when(differs(b, g, mb, mg))
        def _():
            greet(barrier, b, g)

        return carry

    lax.fori_loop(0, 16, say, 0)

    raw[...] = jnp.zeros_like(raw)
    for c in range(3):
        raw[9 * c : 9 * c + 9, 0:16] = points_ref[c]
    for a in range(QP):
        raw[FV + 9 * a : FV + 9 * a + 9, 0:16] = extract_ref[a]
    raw[FC : FC + 9, 0:16] = conn_ref[...].astype(jnp.float32).T
    made = jnp.dot(map_ref[...], raw[...], precision=EXACT, preferred_element_type=jnp.float32)
    record[...] = made.T[0:16, :]

    own_dest = lambda j: pair_device(block, j)

    def count(j, total):
        b, g = own_dest(j)
        return total + jnp.where(differs(b, g, mb, mg), 1, 0)

    gather_greetings(barrier, lax.fori_loop(0, 16, count, 0))

    def slot_of(j):
        diag_pair = j == block
        return jnp.where(diag_pair, block // BLK, jnp.where(block > j, 0, 1))

    def copy(j):
        b, g = own_dest(j)
        slot = slot_of(j)
        return pltpu.make_async_remote_copy(
            src_ref=record,
            dst_ref=out_ref.at[slot, pl.ds(16 * place, 16), :],
            send_sem=send_sem.at[j],
            recv_sem=recv_sem.at[slot * 8 + place],
            device_id=(b, g),
            device_id_type=MESH,
        )

    def send(j, carry):
        b, g = own_dest(j)
        away = differs(b, g, mb, mg)

        @pl.when(away)
        def _():
            copy(j).start()

        @pl.when(jnp.logical_not(away))
        def _():
            out_ref[slot_of(j), pl.ds(pl.multiple_of(16 * place, 16), 16), :] = record[...]

        return carry

    lax.fori_loop(0, 16, send, 0)

    def finish(n, carry):
        b, g = source(n)

        @pl.when(differs(b, g, mb, mg))
        def _():
            pltpu.make_async_remote_copy(
                src_ref=record,
                dst_ref=out_ref.at[n // 8, pl.ds(16 * (n % 8), 16), :],
                send_sem=send_sem.at[n],
                recv_sem=recv_sem.at[n],
                device_id=(b, g),
                device_id_type=MESH,
            ).wait_recv()

        db, dg = own_dest(n)

        @pl.when(differs(db, dg, mb, mg))
        def _():
            copy(n).wait_send()

        return carry

    lax.fori_loop(0, 16, finish, 0)


def gather(conn, extract, points):
    vmem = pl.BlockSpec(memory_space=pltpu.VMEM)
    return pl.pallas_call(
        gather_kernel,
        out_shape=jax.ShapeDtypeStruct((2, TB, TB), jnp.float32),
        in_specs=[vmem] * 4,
        out_specs=vmem,
        scratch_shapes=[
            pltpu.VMEM((TB, TB), jnp.float32),
            pltpu.VMEM((16, TB), jnp.float32),
            pltpu.SemaphoreType.DMA((16,)),
            pltpu.SemaphoreType.DMA((16,)),
        ],
        compiler_params=pltpu.CompilerParams(
            collective_id=0, has_side_effects=True, vmem_limit_bytes=VMEM_LIMIT
        ),
        name="gather_elements",
    )(jnp.asarray(field_map()), conn, extract, points)


def split(value):
    high = value.astype(jnp.bfloat16)
    return high, (value - high.astype(jnp.float32)).astype(jnp.bfloat16)


def build_phi(fields, start, weigh, high_ref, low_ref):
    rows = 32
    for jx in range(6):
        iota = lax.broadcasted_iota(jnp.int32, (rows, TB), 0).astype(jnp.float32) + float(rows * jx)
        sums = [jnp.zeros((rows, TB), jnp.float32) for _ in range(QP)]
        for a in range(QP):
            target = fields[FC + a : FC + a + 1, :] - start
            target = jnp.where(target < 0.0, target + float(M), target)
            hit = jnp.broadcast_to(target, (rows, TB)) == iota
            for k in range(QP):
                value = fields[FV + k * QP + a : FV + k * QP + a + 1, :]
                sums[k] = jnp.where(hit, jnp.broadcast_to(value, (rows, TB)), sums[k])
        for k in range(QP):
            value = weigh(sums[k], k)
            high, low = split(value)
            high_ref[rows * jx : rows * (jx + 1), TB * k : TB * (k + 1)] = high
            low_ref[rows * jx : rows * (jx + 1), TB * k : TB * (k + 1)] = low


def nt(a, b):
    return lax.dot_general(a, b, (((1,), (1,)), ((), ())), preferred_element_type=jnp.float32)


def nn(a, b):
    return lax.dot_general(a, b, (((1,), (0,)), ((), ())), preferred_element_type=jnp.float32)


def pair_kernel(
    rec_ref, x_ref, total_ref, fields, phi_hi, phi_lo, splat, kern, pot_hi, pot_lo, col_sum, row_sum
):
    mb, mg = here()
    hi, lo, diag = own_pair(mb, mg)
    for slot in range(2):
        fields[slot] = rec_ref[slot].T
    for slot, block in ((0, hi), (1, lo)):
        start = (block * TB).astype(jnp.float32)
        view = fields.at[slot]
        build_phi(
            view,
            start,
            lambda v, k: v * jnp.broadcast_to(view[FW + k : FW + k + 1, :], v.shape),
            phi_hi.at[slot],
            phi_lo.at[slot],
        )
        phi_hi[slot, AUG:WIN, :] = jnp.zeros((WIN - AUG, PTS), jnp.bfloat16)
        phi_lo[slot, AUG:WIN, :] = jnp.zeros((WIN - AUG, PTS), jnp.bfloat16)
        for k in range(QP):
            first = lax.broadcasted_iota(jnp.int32, (16, TB), 0) == 0
            weight = jnp.broadcast_to(view[FW + k : FW + k + 1, :], (16, TB))
            high, low = split(jnp.where(first, weight, 0.0))
            phi_hi[slot, AUG : AUG + 16, TB * k : TB * (k + 1)] = high
            phi_lo[slot, AUG : AUG + 16, TB * k : TB * (k + 1)] = low
    total_ref[...] = jnp.zeros_like(total_ref)
    x_ref[1] = jnp.zeros((WIN, WIN), jnp.float32)

    def run(r, carry):
        p_slot = jnp.where(diag, r, 0)
        q_slot = jnp.where(diag, r, 1)
        col_sum[...] = jnp.zeros_like(col_sum)

        def row_chunk(i, carry):
            record = rec_ref[p_slot]

            lane = lax.broadcasted_iota(jnp.int32, (TB, TB), 1)
            for n, base in ((0, FX), (1, FY), (2, FW)):
                picked = jnp.sum(jnp.where(lane == base + i, record, 0.0), axis=1, keepdims=True)
                scaled = picked * (float(EX) / 2.0) if n < 2 else picked * KERNEL_GAIN
                splat[n] = jnp.broadcast_to(scaled, (TB, TB))

            def col_chunk(j, carry):
                wanted = jnp.logical_or(jnp.logical_not(diag), j >= i)

                @pl.when(jnp.logical_not(wanted))
                def _():
                    kern[:, pl.ds(pl.multiple_of(j * TB, TB), TB)] = jnp.zeros((TB, TB), jnp.bfloat16)

                @pl.when(wanted)
                def _():
                    factor = jnp.where(jnp.logical_and(diag, j == i), 0.5, 1.0)
                    qx = fields[q_slot, pl.ds(FX + j, 1), :] * (float(EX) / 2.0)
                    qy = fields[q_slot, pl.ds(FY + j, 1), :] * (float(EX) / 2.0)
                    gap_x = jnp.abs(splat[0] - qx)
                    gap_x = jnp.minimum(gap_x, jnp.abs(float(EX) / 2.0 - gap_x))
                    gap_y = jnp.abs(splat[1] - qy)
                    gap_y = jnp.minimum(gap_y, jnp.abs(float(EY) / 2.0 - gap_y))
                    base = 1.0 + (gap_x * gap_x + gap_y * gap_y)
                    root = lax.rsqrt(base)
                    square = root * root
                    value = factor * (square * square * lax.rsqrt(root))
                    kern[:, pl.ds(pl.multiple_of(j * TB, TB), TB)] = value.astype(jnp.bfloat16)
                    weighed = jnp.sum(value * splat[2], axis=0, keepdims=True)
                    col_sum[pl.ds(j, 1), :] += weighed

                return carry

            lax.fori_loop(0, QP, col_chunk, 0)
            block = kern[...]
            pot = nt(block, phi_hi[q_slot]) + nt(block, phi_lo[q_slot])
            row_sum[pl.ds(i, 1), :] = pot[:, TB:WIN].T[AUG - TB : AUG - TB + 1, :] * KERNEL_GAIN
            high, low = split(pot)
            pot_hi[pl.ds(pl.multiple_of(i * TB, TB), TB), :] = high
            pot_lo[pl.ds(pl.multiple_of(i * TB, TB), TB), :] = low
            return carry

        lax.fori_loop(0, QP, row_chunk, 0)
        inside = jnp.logical_and(
            lax.broadcasted_iota(jnp.int32, (WIN, WIN), 0) < AUG,
            lax.broadcasted_iota(jnp.int32, (WIN, WIN), 1) < AUG,
        )
        x_ref[r] = jnp.where(
            inside,
            KERNEL_GAIN
            * (
                nn(phi_hi[p_slot], pot_hi[...])
                + nn(phi_lo[p_slot], pot_hi[...])
                + nn(phi_hi[p_slot], pot_lo[...])
            ),
            0.0,
        )
        total_ref[p_slot, 0:QP, :] += row_sum[0:QP, :]
        total_ref[q_slot, 0:QP, :] += col_sum[0:QP, :]
        return carry

    lax.fori_loop(0, jnp.where(diag, 2, 1), run, 0)


def pair_work(records):
    vmem = pl.BlockSpec(memory_space=pltpu.VMEM)
    return pl.pallas_call(
        pair_kernel,
        out_shape=(
            jax.ShapeDtypeStruct((2, WIN, WIN), jnp.float32),
            jax.ShapeDtypeStruct((2, 16, TB), jnp.float32),
        ),
        in_specs=[vmem],
        out_specs=(vmem, vmem),
        scratch_shapes=[
            pltpu.VMEM((2, TB, TB), jnp.float32),
            pltpu.VMEM((2, WIN, PTS), jnp.bfloat16),
            pltpu.VMEM((2, WIN, PTS), jnp.bfloat16),
            pltpu.VMEM((3, TB, TB), jnp.float32),
            pltpu.VMEM((TB, PTS), jnp.bfloat16),
            pltpu.VMEM((PTS, WIN), jnp.bfloat16),
            pltpu.VMEM((PTS, WIN), jnp.bfloat16),
            pltpu.VMEM((16, TB), jnp.float32),
            pltpu.VMEM((16, TB), jnp.float32),
        ],
        compiler_params=pltpu.CompilerParams(vmem_limit_bytes=VMEM_LIMIT),
        name="pair_blocks",
    )(records)


def totals_kernel(total_ref, out_ref, send_sem, recv_sem):
    mb, mg = here()
    hi, lo, diag = own_pair(mb, mg)
    barrier = pltpu.get_barrier_semaphore()

    def copy(slot):
        mine, other = (hi, lo) if slot == 0 else (lo, hi)
        return pltpu.make_async_remote_copy(
            src_ref=total_ref.at[slot],
            dst_ref=out_ref.at[mine // BLK, other],
            send_sem=send_sem.at[slot],
            recv_sem=recv_sem.at[mine // BLK, other],
            device_id=(mine % BLK, mine % BLK),
            device_id_type=MESH,
        )

    @pl.when(diag)
    def _():
        def say(n, carry):
            block, other = mg + (n // 16) * BLK, n % 16

            @pl.when(block != other)
            def _():
                b, g = pair_device(block, other)
                greet(barrier, b, g)

            return carry

        lax.fori_loop(0, 32, say, 0)
        for slot in range(2):
            out_ref[slot, mg + slot * BLK] = total_ref[slot]

        def take(n, carry):
            half, other = n // 16, n % 16

            @pl.when(mg + half * BLK != other)
            def _():
                pltpu.make_async_remote_copy(
                    src_ref=total_ref.at[0],
                    dst_ref=out_ref.at[half, other],
                    send_sem=send_sem.at[0],
                    recv_sem=recv_sem.at[half, other],
                    device_id=(mb, mg),
                    device_id_type=MESH,
                ).wait_recv()

            return carry

        lax.fori_loop(0, 32, take, 0)

    @pl.when(jnp.logical_not(diag))
    def _():
        pl.semaphore_wait(barrier, 2)
        for slot in range(2):
            copy(slot).start()
        for slot in range(2):
            copy(slot).wait_send()


def totals_exchange(total):
    vmem = pl.BlockSpec(memory_space=pltpu.VMEM)
    return pl.pallas_call(
        totals_kernel,
        out_shape=jax.ShapeDtypeStruct((2, 16, 16, TB), jnp.float32),
        in_specs=[vmem],
        out_specs=vmem,
        scratch_shapes=[pltpu.SemaphoreType.DMA((2,)), pltpu.SemaphoreType.DMA((2, 16))],
        compiler_params=pltpu.CompilerParams(
            collective_id=1, has_side_effects=True, vmem_limit_bytes=VMEM_LIMIT
        ),
        name="send_totals",
    )(total)


def pieces_kernel(rec_ref, x_ref, parts_ref, out_ref, fields, phi_hi, phi_lo):
    mb, mg = here()
    hi, lo, diag = own_pair(mb, mg)

    @pl.when(jnp.logical_not(diag))
    def _():
        for n in range(4):
            u, v = n // 2, n % 2
            piece = -x_ref[0, TB * u : TB * (u + 1), TB * v : TB * (v + 1)]
            row, col = (hi + u) % 16, (lo + v) % 16
            if u == 0 and v == 0:
                out_ref[n] = piece
            else:
                other = piece.T
                out_ref[n] = jnp.where(row < col, 0.0, piece) + jnp.where(row > col, 0.0, other)

    @pl.when(diag)
    def _():
        for r in range(2):
            block = mg + BLK * r
            fields[...] = rec_ref[r].T
            build_phi(fields, (block * TB).astype(jnp.float32), lambda v, k: v, phi_hi, phi_lo)
            for ref in (phi_hi, phi_lo):
                ref[AUG:WIN, :] = jnp.zeros((WIN - AUG, PTS), jnp.bfloat16)
            gain = jnp.sum(parts_ref[r], axis=0)
            mass = jnp.zeros((WIN, WIN), jnp.float32)
            for k in range(QP):
                lanes = slice(TB * k, TB * (k + 1))
                left = phi_hi[:, lanes].astype(jnp.float32) + phi_lo[:, lanes].astype(jnp.float32)
                factor = fields[FW + k : FW + k + 1, :] * (MASS_SHIFT + gain[k : k + 1, :])
                high, low = split(left * factor)
                mass += (
                    nt(high, phi_hi[:, lanes]) + nt(low, phi_hi[:, lanes]) + nt(high, phi_lo[:, lanes])
                )
            x = x_ref[r]
            for n, (u, v) in enumerate(((0, 0), (1, 0), (1, 1))):
                one = x[TB * u : TB * (u + 1), TB * v : TB * (v + 1)]
                two = x[TB * v : TB * (v + 1), TB * u : TB * (u + 1)]
                whole = mass[TB * u : TB * (u + 1), TB * v : TB * (v + 1)] - one - two.T
                if u != v and r == 1:
                    flip = block == 15
                    whole = jnp.where(flip, 0.0, whole) + jnp.where(flip, whole.T, 0.0)
                out_ref[3 * r + n] = whole


def make_pieces(records, x, parts):
    vmem = pl.BlockSpec(memory_space=pltpu.VMEM)
    return pl.pallas_call(
        pieces_kernel,
        out_shape=jax.ShapeDtypeStruct((6, TB, TB), jnp.float32),
        in_specs=[vmem] * 3,
        out_specs=vmem,
        scratch_shapes=[
            pltpu.VMEM((TB, TB), jnp.float32),
            pltpu.VMEM((WIN, PTS), jnp.bfloat16),
            pltpu.VMEM((WIN, PTS), jnp.bfloat16),
        ],
        compiler_params=pltpu.CompilerParams(vmem_limit_bytes=VMEM_LIMIT),
        name="make_pieces",
    )(records, x, parts)


def piece_target(n, hi, lo, diag, g):
    u, v = n // 2, n % 2
    row, col = (hi + u) % 16, (lo + v) % 16
    slot = jnp.where(row == col, 1, jnp.where(row > col, 2 * u + v, 2 * v + u))
    r, m = n // 3, n % 3
    block = g + BLK * r
    after = (block + 1) % 16
    drow = jnp.where(m == 0, block, jnp.where(m == 1, jnp.maximum(block, after), after))
    dcol = jnp.where(m == 0, block, jnp.where(m == 1, jnp.minimum(block, after), after))
    dslot = jnp.where(m == 0, 0, jnp.where(m == 1, jnp.where(block == 15, 1, 2), 3))
    big = jnp.where(diag, drow, jnp.maximum(row, col))
    small = jnp.where(diag, dcol, jnp.minimum(row, col))
    there = jnp.where(diag, 6, 4) > n
    return small % BLK, big, small // BLK, jnp.where(diag, dslot, slot), there


def piece_source(t, s, b, g):
    row, col = g, b + BLK * t
    there = jnp.logical_and(row >= col, jnp.logical_not(jnp.logical_and(row == col, s == 2)))
    sb, sg = pair_device((row - s // 2 + 16) % 16, (col - s % 2 + 16) % 16)
    return sb, sg, there


def reduce_kernel(piece_ref, out_ref, landed, send_sem, recv_sem):
    mb, mg = here()
    hi, lo, diag = own_pair(mb, mg)
    barrier = pltpu.get_barrier_semaphore()

    def say(n, carry):
        sb, sg, there = piece_source(n // 4, n % 4, mb, mg)

        @pl.when(jnp.logical_and(there, differs(sb, sg, mb, mg)))
        def _():
            greet(barrier, sb, sg)

        return carry

    lax.fori_loop(0, 8, say, 0)

    def count(n, total):
        b, g, t, s, there = piece_target(n, hi, lo, diag, mg)
        return total + jnp.where(jnp.logical_and(there, differs(b, g, mb, mg)), 1, 0)

    gather_greetings(barrier, lax.fori_loop(0, 6, count, 0))

    def copy(n):
        b, g, t, s, there = piece_target(n, hi, lo, diag, mg)
        return pltpu.make_async_remote_copy(
            src_ref=piece_ref.at[n],
            dst_ref=landed.at[t, s],
            send_sem=send_sem.at[n],
            recv_sem=recv_sem.at[t, s],
            device_id=(b, g),
            device_id_type=MESH,
        )

    def send(n, carry):
        b, g, t, s, there = piece_target(n, hi, lo, diag, mg)
        away = differs(b, g, mb, mg)

        @pl.when(jnp.logical_and(there, away))
        def _():
            copy(n).start()

        @pl.when(jnp.logical_and(there, jnp.logical_not(away)))
        def _():
            landed[t, s] = piece_ref[n]

        return carry

    lax.fori_loop(0, 6, send, 0)
    out_ref[...] = jnp.zeros_like(out_ref)

    def take(n, carry):
        t, s = n // 4, n % 4
        sb, sg, there = piece_source(t, s, mb, mg)

        @pl.when(there)
        def _():
            @pl.when(differs(sb, sg, mb, mg))
            def _():
                pltpu.make_async_remote_copy(
                    src_ref=piece_ref.at[0],
                    dst_ref=landed.at[t, s],
                    send_sem=send_sem.at[0],
                    recv_sem=recv_sem.at[t, s],
                    device_id=(sb, sg),
                    device_id_type=MESH,
                ).wait_recv()

            out_ref[t] += landed[t, s]

        return carry

    lax.fori_loop(0, 8, take, 0)

    def drain(n, carry):
        b, g, t, s, there = piece_target(n, hi, lo, diag, mg)

        @pl.when(jnp.logical_and(there, differs(b, g, mb, mg)))
        def _():
            copy(n).wait_send()

        return carry

    lax.fori_loop(0, 6, drain, 0)


def reduce_pieces(pieces):
    vmem = pl.BlockSpec(memory_space=pltpu.VMEM)
    return pl.pallas_call(
        reduce_kernel,
        out_shape=jax.ShapeDtypeStruct((2, TB, TB), jnp.float32),
        in_specs=[vmem],
        out_specs=vmem,
        scratch_shapes=[
            pltpu.VMEM((2, 4, TB, TB), jnp.float32),
            pltpu.SemaphoreType.DMA((6,)),
            pltpu.SemaphoreType.DMA((2, 4)),
        ],
        compiler_params=pltpu.CompilerParams(
            collective_id=2, has_side_effects=True, vmem_limit_bytes=VMEM_LIMIT
        ),
        name="sum_pieces",
    )(pieces)


def panel_kernel(tile_ref, out_ref, send_sem, recv_sem):
    mb, mg = here()
    barrier = pltpu.get_barrier_semaphore()
    first = mb == 0
    root = jnp.logical_and(first, mg == 0)
    relay = jnp.logical_and(mg >= 1, mb == mg % BLK)

    def wants(t):
        col = mb + BLK * t
        return jnp.logical_and(col >= 1, mg > col)

    @pl.when(jnp.logical_not(first))
    def _():
        greet(barrier, 0, mg)

    @pl.when(jnp.logical_and(first, mg > 0))
    def _():
        greet(barrier, 0, 0)

    for t in range(2):
        @pl.when(wants(t))
        def _(t=t):
            greet(barrier, mb, mb + BLK * t)

    expected = (
        jnp.where(first, BLK - 1, 0)
        + jnp.where(root, GRID - 1, 0)
        + jnp.where(relay, GRID - 1 - mg, 0)
    )
    gather_greetings(barrier, expected)

    def copy(source, n, sem, b, g):
        return pltpu.make_async_remote_copy(
            src_ref=source,
            dst_ref=out_ref.at[n],
            send_sem=send_sem.at[sem],
            recv_sem=recv_sem.at[n],
            device_id=(b, g),
            device_id_type=MESH,
        )

    @pl.when(root)
    def _():
        out_ref[0] = tile_ref[0]

    def root_send(g, carry):
        copy(tile_ref.at[0], 0, g, 0, g).start()
        return carry

    @pl.when(root)
    def _():
        lax.fori_loop(1, GRID, root_send, 0)

    @pl.when(first)
    def _():
        out_ref[1] = tile_ref[0]

        def row_send(b, carry):
            copy(tile_ref.at[0], 1, 16 + b, b, mg).start()
            return carry

        lax.fori_loop(1, BLK, row_send, 0)

    @pl.when(jnp.logical_not(first))
    def _():
        copy(tile_ref.at[0], 1, 0, mb, mg).wait_recv()

    def relay_copy(g):
        return copy(out_ref.at[1], 2 + mg // BLK, 40 + g, mb, g)

    @pl.when(relay)
    def _():
        def relay_send(g, carry):
            relay_copy(g).start()
            return carry

        lax.fori_loop(mg + 1, GRID, relay_send, 0)

    @pl.when(jnp.logical_not(root))
    def _():
        copy(tile_ref.at[0], 0, 0, mb, mg).wait_recv()

    @pl.when(first)
    def _():
        def head_send(b, carry):
            copy(out_ref.at[0], 0, 24 + b, b, mg).start()
            return carry

        lax.fori_loop(1, BLK, head_send, 0)

    for t in range(2):
        col = mb + BLK * t

        @pl.when(mg == col)
        def _(t=t):
            out_ref[2 + t] = out_ref[1]

        @pl.when(wants(t))
        def _(t=t):
            copy(tile_ref.at[0], 2 + t, 0, mb, mg).wait_recv()

        @pl.when(jnp.logical_not(jnp.logical_or(mg == col, wants(t))))
        def _(t=t):
            out_ref[2 + t] = jnp.zeros((TB, TB), jnp.float32)

    @pl.when(root)
    def _():
        def root_wait(g, carry):
            copy(tile_ref.at[0], 0, g, 0, g).wait_send()
            return carry

        lax.fori_loop(1, GRID, root_wait, 0)

    @pl.when(first)
    def _():
        def row_wait(b, carry):
            copy(tile_ref.at[0], 1, 16 + b, b, mg).wait_send()
            copy(out_ref.at[0], 0, 24 + b, b, mg).wait_send()
            return carry

        lax.fori_loop(1, BLK, row_wait, 0)

    @pl.when(relay)
    def _():
        def relay_wait(g, carry):
            relay_copy(g).wait_send()
            return carry

        lax.fori_loop(mg + 1, GRID, relay_wait, 0)


def share_panel(tiles):
    vmem = pl.BlockSpec(memory_space=pltpu.VMEM)
    return pl.pallas_call(
        panel_kernel,
        out_shape=jax.ShapeDtypeStruct((4, TB, TB), jnp.float32),
        in_specs=[vmem],
        out_specs=vmem,
        scratch_shapes=[pltpu.SemaphoreType.DMA((56,)), pltpu.SemaphoreType.DMA((4,))],
        compiler_params=pltpu.CompilerParams(
            collective_id=3, has_side_effects=True, vmem_limit_bytes=VMEM_LIMIT
        ),
        name="share_panel",
    )(tiles)


def eliminate(work):
    for kb in range(TB // 8):
        lo = 8 * kb
        panel = work[lo : lo + 8, :]
        row_at = lax.broadcasted_iota(jnp.int32, (8, 1), 0)
        for j in range(8):
            col = panel[:, lo + j : lo + j + 1]
            pivot = panel[j : j + 1, :]
            scale = lax.rsqrt(pivot[:, lo + j : lo + j + 1])
            done = pivot * scale
            panel = jnp.where(
                row_at == j, done, panel - jnp.where(row_at > j, col * scale, 0.0) * done
            )
        work[lo : lo + 8, :] = panel
        if lo + 8 < TB:
            work[lo + 8 : TB, :] -= lax.dot_general(
                panel[:, lo + 8 : TB],
                panel,
                (((0,), (0,)), ((), ())),
                precision=EXACT,
                preferred_element_type=jnp.float32,
            )


def factor_kernel(panel_ref, tile_ref, out_ref, work):
    mb, mg = here()
    head = panel_ref[0]
    row = lax.broadcasted_iota(jnp.int32, (TB, TB), 0)
    col = lax.broadcasted_iota(jnp.int32, (TB, TB), 1)
    work[:, 0:TB] = 0.5 * (head + head.T)
    work[:, TB:WIN] = jnp.where(row == col, 1.0, 0.0)
    eliminate(work)
    lower = jnp.where(row >= col, work[:, 0:TB].T, 0.0)
    inverse = jnp.where(row >= col, work[:, TB:WIN], 0.0)

    def solve(n):
        return lax.dot_general(
            panel_ref[n],
            inverse,
            (((1,), (1,)), ((), ())),
            precision=EXACT,
            preferred_element_type=jnp.float32,
        )

    left = jnp.where(mg == 0, lower, solve(1))
    for t in range(2):
        tile_col = mb + BLK * t
        update = lax.dot_general(
            left,
            solve(2 + t),
            (((1,), (1,)), ((), ())),
            precision=EXACT,
            preferred_element_type=jnp.float32,
        )
        value = jnp.where(tile_col == 0, left, tile_ref[t] - update)
        keep = mg * TB + row >= tile_col * TB + col
        out_ref[0, :, t, :] = jnp.where(keep, value, 0.0)


def factor(panel, tiles):
    vmem = pl.BlockSpec(memory_space=pltpu.VMEM)
    return pl.pallas_call(
        factor_kernel,
        out_shape=jax.ShapeDtypeStruct((1, TB, 2, TB), jnp.float32),
        in_specs=[vmem] * 2,
        out_specs=vmem,
        scratch_shapes=[pltpu.VMEM((TB, WIN), jnp.float32)],
        compiler_params=pltpu.CompilerParams(vmem_limit_bytes=VMEM_LIMIT),
        name="factor_tiles",
    )(panel, tiles)


def shards(conn, extract, points):
    records = gather(conn, extract, points)
    x, total = pair_work(records)
    parts = totals_exchange(total)
    pieces = make_pieces(records, x, parts)
    tiles = reduce_pieces(pieces)
    panel = share_panel(tiles)
    return factor(panel, tiles)


def solution(mesh):
    in_specs = (
        P(("blk", "grid"), None),
        P(None, None, ("blk", "grid")),
        P(None, None, ("blk", "grid")),
    )
    out_specs = P(None, "grid", None, "blk")
    return jax.shard_map(shards, mesh=mesh, in_specs=in_specs, out_specs=out_specs, check_vma=False)
```

time: 1190 us -> 98.5 us (0.08)
  blocking collectives: 542 us -> 0 us
  waiting for transfers between devices: 335 us -> 0 us
  local copies, waits for them, and re-layouts: 120 us -> 2.46 us
  other arithmetic: 98.2 us -> 0 us
  Pallas kernels: 0 us -> 95.8 us
  matrix products: 70.7 us -> 0 us
  between operations: 13.4 us -> 0.05 us
    all_gather x3 -> x0, blocking collectives: 542 us -> none  [the longest x1 186 us: shards(): lax.all_gather(points_flat, ('blk', 'grid'), axis=1, tiled=True)]
    unnamed x4 -> x0, waiting for transfers between devices: 216 us -> none
    pallas_call x0 -> x7, Pallas kernels: none -> 95.8 us  [the longest x1 26.9 us: share_panel(): pl.pallas_call(panel_kernel, out_shape=jax.ShapeDtypeStruct((4, TB, TB),...]
    dot_general x51 -> x0, matrix products: 69.7 us -> none  [the longest x16 38.3 us: step(): jnp.dot(kernel_block, trial_phi, precision=lax.Precision.HIGHEST, preferr...]
    psum x1 -> x0, waiting for transfers between devices: 67 us -> none  [spread(): return lax.psum(jnp.where(mine, array, jnp.zeros_like(array)), axis)]
    all_gather x1 -> x0, waiting for transfers between devices: 51.9 us -> none  [shards(): panel_tiles = lax.all_gather(mine, 'grid', axis=0, tiled=True)]
    dynamic_update_slice x16 -> x0, local copies, waits for them, and re-layouts: 27.4 us -> none  [step(): lax.dynamic_update_slice_in_dim(potential_wide, current + block, offset, 1)]
    reshape x40 -> x0, local copies, waits for them, and re-layouts: 26.7 us -> none  [the longest x1 18.2 us: shards(): term = placed.reshape(blk_size * grid_size, -1)]
  transfers between devices with their start and end apart: 3 -> 0, of which waited for: 3 -> 0; matrix products, arithmetic and copies ran while one was open for 0% -> 0% of each run, Pallas kernels for 0% -> 0%
where the time goes in v1:
time: 98.5 us; the launch traced here: 98.3 us
  Pallas kernels  95.8 us (97%)
  local copies, waits for them, and re-layouts  2.46 us (2%)
    pallas_call x1, Pallas kernels, share_panel(): pl.pallas_call(panel_kernel, out_shape=jax.ShapeDtypeStruct((4, TB, TB),...  26.9 us
    pallas_call x1, Pallas kernels, factor(): pl.pallas_call(factor_kernel, out_shape=jax.ShapeDtypeStruct((1, TB, 2, T...  16.9 us
    pallas_call x1, Pallas kernels, reduce_pieces(): pl.pallas_call(reduce_kernel, out_shape=jax.ShapeDtypeStruct((2, TB, TB),...  16 us
    pallas_call x1, Pallas kernels, pair_work(): pl.pallas_call(pair_kernel, out_shape=(jax.ShapeDtypeStruct((2, WIN, WIN)...  14.4 us
    pallas_call x1, Pallas kernels, totals_exchange(): pl.pallas_call(totals_kernel, out_shape=jax.ShapeDtypeStruct((2, 16, 16,...  13.3 us
    pallas_call x1, Pallas kernels, gather(): pl.pallas_call(gather_kernel, out_shape=jax.ShapeDtypeStruct((2, TB, TB),...  8.14 us
    unnamed x7, local copies, waits for them, and re-layouts  2.46 us

profile of v1, /device:TPU:127, one launch (start us, length us, event | category | flops | bytes accessed | tf_op | source)
XLA Modules:
  0.0 98.3 jit_solution(13280467363378735952)
XLA Ops:
  0.0 0.0 copy-start.2
  0.0 0.7 copy.5.points_ref
  0.7 0.0 copy-done.2
  0.7 0.0 copy-start
  0.7 0.9 copy-done
  1.6 0.0 copy-start.1
  1.6 0.8 copy-done.1
  2.5 8.1 %gather_elements.1.rec_ref = f32[2,128,128]{2,1,0:T(8,128)S(1)} custom-call(f32[128,128]{1,0:T(8,128)S(1)} %copy-done.1, s32[16,9]{1,0:T(8,128)S(1)} %copy-done.2, f32[9,9,16]{2,1,0:T(8,128)S(1)} %copy-done, f32[3,9,16]{2,1,0:T(8,128)S(1)} %copy.5.points_ref), custom_call_target="tpu_custom_call" | custom-call | tf_op jit(solution)/shard_map/gather_elements/pallas_call | solution.py:193
  10.6 14.4 %pair_blocks.1 = (f32[2,256,256]{2,1,0:T(8,128)S(1)}, f32[2,16,128]{2,1,0:T(8,128)S(1)}) custom-call(f32[2,128,128]{2,1,0:T(8,128)S(1)} %gather_elements.1.rec_ref), custom_call_target="tpu_custom_call" | custom-call | tf_op jit(solution)/shard_map/pair_blocks/pallas_call | solution.py:344
  25.0 13.3 %send_totals.1.parts_ref = f32[2,16,16,128]{3,2,1,0:T(8,128)S(1)} custom-call(f32[2,16,128]{2,1,0:T(8,128)S(1)} %get-tuple-element.8.total_ref), custom_call_target="tpu_custom_call" | custom-call | tf_op jit(solution)/shard_map/send_totals/pallas_call | solution.py:429
  38.3 0.1 make_pieces.1.piece_ref
  38.5 16.0 %sum_pieces.1.tile_ref = f32[2,128,128]{2,1,0:T(8,128)S(1)} custom-call(f32[6,128,128]{2,1,0:T(8,128)S(1)} %make_pieces.1.piece_ref), custom_call_target="tpu_custom_call" | custom-call | tf_op jit(solution)/shard_map/sum_pieces/pallas_call | solution.py:614
  54.5 26.9 %share_panel.1.panel_ref = f32[4,128,128]{2,1,0:T(8,128)S(1)} custom-call(f32[2,128,128]{2,1,0:T(8,128)S(1)} %sum_pieces.1.tile_ref), custom_call_target="tpu_custom_call" | custom-call | tf_op jit(solution)/shard_map/share_panel/pallas_call | solution.py:764
  81.4 16.9 %factor_tiles.1 = f32[1,128,2,128]{3,2,1,0:T(2,128)} custom-call(f32[4,128,128]{2,1,0:T(8,128)S(1)} %share_panel.1.panel_ref, f32[2,128,128]{2,1,0:T(8,128)S(1)} %sum_pieces.1.tile_ref), custom_call_target="tpu_custom_call" | custom-call | tf_op jit(solution)/shard_map/factor_tiles/pallas_call | solution.py:838
Async XLA Ops:
  0.0 0.7 copy-start.2
  0.7 0.9 copy-start
  1.6 0.8 copy-start.1

commit v2 on v1

--- a/solution.py
+++ b/solution.py
@@ -54,7 +54,7 @@
     for k in range(QP):
         for a in range(QP):
             for b in range(QP):
-                table[FV + k * QP + a, FV + a * QP + b] = bern[k, b]
+                table[FV + a * QP + k, FV + a * QP + b] = bern[k, b]
     return table
 
 
@@ -213,20 +213,39 @@
     return high, (value - high.astype(jnp.float32)).astype(jnp.bfloat16)
 
 
-def build_phi(fields, start, weigh, high_ref, low_ref):
-    rows = 32
+def build_phi(fields, start, weigh, spread, high_ref, low_ref):
+    lane = lax.broadcasted_iota(jnp.int32, (QP, TB), 1)
+    cell_y = lane % EY
+    cell_x = lane // EY
+    target = fields[FC : FC + QP, :].astype(jnp.int32) - start
+    target = jnp.where(target < 0, target + M, target)
+    place = 3 * (target // EY - cell_x) + (target % EY - cell_y + EY) % EY
+    weight = fields[FW : FW + QP, :]
+    slots = [jnp.zeros((QP, TB), jnp.float32) for _ in range(QP)]
+    for a in range(QP):
+        value = fields[FV + QP * a : FV + QP * (a + 1), :]
+        if weigh:
+            value = value * weight
+        here_a = jnp.broadcast_to(place[a : a + 1, :], (QP, TB))
+        for n in range(QP):
+            slots[n] = jnp.where(here_a == n, value, slots[n])
     for jx in range(6):
-        iota = lax.broadcasted_iota(jnp.int32, (rows, TB), 0).astype(jnp.float32) + float(rows * jx)
-        sums = [jnp.zeros((rows, TB), jnp.float32) for _ in range(QP)]
-        for a in range(QP):
-            target = fields[FC + a : FC + a + 1, :] - start
-            target = jnp.where(target < 0.0, target + float(M), target)
-            hit = jnp.broadcast_to(target, (rows, TB)) == iota
-            for k in range(QP):
-                value = fields[FV + k * QP + a : FV + k * QP + a + 1, :]
-                sums[k] = jnp.where(hit, jnp.broadcast_to(value, (rows, TB)), sums[k])
+        for t in range(3):
+            row = jnp.zeros((QP, TB), jnp.float32)
+            for step in range(3):
+                if 0 <= jx - step <= 3:
+                    row = jnp.where(cell_x == jx - step, slots[3 * step + t], row)
+            spread[3 * jx + t, 0:QP, :] = row
+    rows = EY
+    wide_y = lax.broadcasted_iota(jnp.int32, (rows, TB), 1) % EY
+    down_y = lax.broadcasted_iota(jnp.int32, (rows, TB), 0)
+    hits = [(wide_y + t) % EY == down_y for t in range(3)]
+    for jx in range(6):
         for k in range(QP):
-            value = weigh(sums[k], k)
+            value = jnp.zeros((rows, TB), jnp.float32)
+            for t in range(3):
+                line = jnp.broadcast_to(spread[3 * jx + t, k : k + 1, :], (rows, TB))
+                value = jnp.where(hits[t], line, value)
             high, low = split(value)
             high_ref[rows * jx : rows * (jx + 1), TB * k : TB * (k + 1)] = high
             low_ref[rows * jx : rows * (jx + 1), TB * k : TB * (k + 1)] = low
@@ -240,31 +259,32 @@
     return lax.dot_general(a, b, (((1,), (0,)), ((), ())), preferred_element_type=jnp.float32)
 
 
+HALF_X = float(EX) / 4.0
+HALF_Y = float(EY) / 4.0
+
+
 def pair_kernel(
-    rec_ref, x_ref, total_ref, fields, phi_hi, phi_lo, splat, kern, pot_hi, pot_lo, col_sum, row_sum
+    rec_ref, x_ref, total_ref, fields, spread, phi_hi, phi_lo, trial_x, trial_y, splat, kern, pot, col_sum
 ):
     mb, mg = here()
     hi, lo, diag = own_pair(mb, mg)
-    for slot in range(2):
-        fields[slot] = rec_ref[slot].T
+    cell_y = lax.broadcasted_iota(jnp.int32, (QP, TB), 1) % EY
+    first = lax.broadcasted_iota(jnp.int32, (16, TB), 0) == 0
     for slot, block in ((0, hi), (1, lo)):
-        start = (block * TB).astype(jnp.float32)
         view = fields.at[slot]
-        build_phi(
-            view,
-            start,
-            lambda v, k: v * jnp.broadcast_to(view[FW + k : FW + k + 1, :], v.shape),
-            phi_hi.at[slot],
-            phi_lo.at[slot],
-        )
-        phi_hi[slot, AUG:WIN, :] = jnp.zeros((WIN - AUG, PTS), jnp.bfloat16)
-        phi_lo[slot, AUG:WIN, :] = jnp.zeros((WIN - AUG, PTS), jnp.bfloat16)
+        view[...] = rec_ref[slot].T
+        build_phi(view, block * TB, True, spread, phi_hi.at[slot], phi_lo.at[slot])
+        for ref in (phi_hi, phi_lo):
+            ref[slot, AUG:WIN, :] = jnp.zeros((WIN - AUG, PTS), jnp.bfloat16)
         for k in range(QP):
-            first = lax.broadcasted_iota(jnp.int32, (16, TB), 0) == 0
             weight = jnp.broadcast_to(view[FW + k : FW + k + 1, :], (16, TB))
             high, low = split(jnp.where(first, weight, 0.0))
             phi_hi[slot, AUG : AUG + 16, TB * k : TB * (k + 1)] = high
             phi_lo[slot, AUG : AUG + 16, TB * k : TB * (k + 1)] = low
+        trial_x[slot, 0:QP, :] = view[FX : FX + QP, :] * (EX / 2.0) + HALF_X
+        for quarter in range(4):
+            turn = jnp.where(cell_y > 8 * quarter + 8, HALF_Y - 2.0 * HALF_Y, HALF_Y)
+            trial_y[slot, quarter, 0:QP, :] = view[FY : FY + QP, :] * (EX / 2.0) + turn
     total_ref[...] = jnp.zeros_like(total_ref)
     x_ref[1] = jnp.zeros((WIN, WIN), jnp.float32)
 
@@ -273,67 +293,67 @@
         q_slot = jnp.where(diag, r, 1)
         col_sum[...] = jnp.zeros_like(col_sum)
 
-        def row_chunk(i, carry):
-            record = rec_ref[p_slot]
-
-            lane = lax.broadcasted_iota(jnp.int32, (TB, TB), 1)
+        def chunk(i, j):
+            qx = jnp.broadcast_to(trial_x[q_slot, pl.ds(j, 1), :], (8, TB))
+            qy = [
+                jnp.broadcast_to(trial_y[q_slot, quarter, pl.ds(j, 1), :], (8, TB)) for quarter in range(4)
+            ]
+            sums = jnp.zeros((8, TB), jnp.float32)
+            for h in range(8):
+                values = []
+                for n in (2 * h, 2 * h + 1):
+                    rows = slice(8 * n, 8 * n + 8)
+                    gap_x = HALF_X - jnp.abs(splat[0, rows, :] - qx)
+                    gap_y = HALF_Y - jnp.abs(splat[1, rows, :] - qy[n % 4])
+                    root = lax.rsqrt(1.0 + (gap_x * gap_x + gap_y * gap_y))
+                    square = root * root
+                    value = square * square * lax.rsqrt(root)
+                    sums = sums + value * splat[2, rows, :]
+                    values.append(value)
+                kern[TB * i + 16 * h : TB * i + 16 * h + 16, pl.ds(pl.multiple_of(j * TB, TB), TB)] = (
+                    jnp.concatenate(values, axis=0).astype(jnp.bfloat16)
+                )
+            return jnp.sum(sums, axis=0, keepdims=True)
+
+        for i in range(QP):
             for n, base in ((0, FX), (1, FY), (2, FW)):
-                picked = jnp.sum(jnp.where(lane == base + i, record, 0.0), axis=1, keepdims=True)
-                scaled = picked * (float(EX) / 2.0) if n < 2 else picked * KERNEL_GAIN
-                splat[n] = jnp.broadcast_to(scaled, (TB, TB))
-
-            def col_chunk(j, carry):
-                wanted = jnp.logical_or(jnp.logical_not(diag), j >= i)
-
-                @pl.when(jnp.logical_not(wanted))
-                def _():
-                    kern[:, pl.ds(pl.multiple_of(j * TB, TB), TB)] = jnp.zeros((TB, TB), jnp.bfloat16)
-
-                @pl.when(wanted)
-                def _():
-                    factor = jnp.where(jnp.logical_and(diag, j == i), 0.5, 1.0)
-                    qx = fields[q_slot, pl.ds(FX + j, 1), :] * (float(EX) / 2.0)
-                    qy = fields[q_slot, pl.ds(FY + j, 1), :] * (float(EX) / 2.0)
-                    gap_x = jnp.abs(splat[0] - qx)
-                    gap_x = jnp.minimum(gap_x, jnp.abs(float(EX) / 2.0 - gap_x))
-                    gap_y = jnp.abs(splat[1] - qy)
-                    gap_y = jnp.minimum(gap_y, jnp.abs(float(EY) / 2.0 - gap_y))
-                    base = 1.0 + (gap_x * gap_x + gap_y * gap_y)
-                    root = lax.rsqrt(base)
-                    square = root * root
-                    value = factor * (square * square * lax.rsqrt(root))
-                    kern[:, pl.ds(pl.multiple_of(j * TB, TB), TB)] = value.astype(jnp.bfloat16)
-                    weighed = jnp.sum(value * splat[2], axis=0, keepdims=True)
-                    col_sum[pl.ds(j, 1), :] += weighed
-
-                return carry
-
-            lax.fori_loop(0, QP, col_chunk, 0)
-            block = kern[...]
-            pot = nt(block, phi_hi[q_slot]) + nt(block, phi_lo[q_slot])
-            row_sum[pl.ds(i, 1), :] = pot[:, TB:WIN].T[AUG - TB : AUG - TB + 1, :] * KERNEL_GAIN
-            high, low = split(pot)
-            pot_hi[pl.ds(pl.multiple_of(i * TB, TB), TB), :] = high
-            pot_lo[pl.ds(pl.multiple_of(i * TB, TB), TB), :] = low
-            return carry
-
-        lax.fori_loop(0, QP, row_chunk, 0)
+                picked = rec_ref[p_slot, :, base + i : base + i + 1] * (EX / 2.0 if n < 2 else KERNEL_GAIN)
+                splat[n] = jnp.broadcast_to(picked, (TB, TB))
+
+            @pl.when(jnp.logical_not(diag))
+            def _(i=i):
+                def full(j, carry):
+                    col_sum[pl.ds(j, 1), :] += chunk(i, j)
+                    return carry
+
+                lax.fori_loop(0, QP, full, 0, unroll=3)
+
+            @pl.when(diag)
+            def _(i=i):
+                if i > 0:
+                    kern[TB * i : TB * (i + 1), 0 : TB * i] = jnp.zeros((TB, TB * i), jnp.bfloat16)
+                col_sum[i : i + 1, :] += 0.5 * chunk(i, i)
+                here_i = slice(TB * i, TB * (i + 1))
+                kern[here_i, here_i] = kern[here_i, here_i] * 0.5
+
+                def part(j, carry):
+                    col_sum[pl.ds(j, 1), :] += chunk(i, j)
+                    return carry
+
+                lax.fori_loop(i + 1, QP, part, 0)
+
+        pot[...] = nt(kern[...], phi_hi[q_slot]) + nt(kern[...], phi_lo[q_slot])
+        total_ref[q_slot, 0:QP, :] += col_sum[0:QP, :]
+        for i in range(QP):
+            column = pot[TB * i : TB * (i + 1), TB:WIN].T
+            total_ref[p_slot, i : i + 1, :] += column[AUG - TB : AUG - TB + 1, :] * KERNEL_GAIN
+        high, low = split(pot[...])
         inside = jnp.logical_and(
             lax.broadcasted_iota(jnp.int32, (WIN, WIN), 0) < AUG,
             lax.broadcasted_iota(jnp.int32, (WIN, WIN), 1) < AUG,
         )
-        x_ref[r] = jnp.where(
-            inside,
-            KERNEL_GAIN
-            * (
-                nn(phi_hi[p_slot], pot_hi[...])
-                + nn(phi_lo[p_slot], pot_hi[...])
-                + nn(phi_hi[p_slot], pot_lo[...])
-            ),
-            0.0,
-        )
-        total_ref[p_slot, 0:QP, :] += row_sum[0:QP, :]
-        total_ref[q_slot, 0:QP, :] += col_sum[0:QP, :]
+        value = nn(phi_hi[p_slot], high) + nn(phi_lo[p_slot], high) + nn(phi_hi[p_slot], low)
+        x_ref[r] = jnp.where(inside, KERNEL_GAIN * value, 0.0)
         return carry
 
     lax.fori_loop(0, jnp.where(diag, 2, 1), run, 0)
@@ -351,13 +371,14 @@
         out_specs=(vmem, vmem),
         scratch_shapes=[
             pltpu.VMEM((2, TB, TB), jnp.float32),
+            pltpu.VMEM((18, 16, TB), jnp.float32),
             pltpu.VMEM((2, WIN, PTS), jnp.bfloat16),
             pltpu.VMEM((2, WIN, PTS), jnp.bfloat16),
+            pltpu.VMEM((2, 16, TB), jnp.float32),
+            pltpu.VMEM((2, 4, 16, TB), jnp.float32),
             pltpu.VMEM((3, TB, TB), jnp.float32),
-            pltpu.VMEM((TB, PTS), jnp.bfloat16),
-            pltpu.VMEM((PTS, WIN), jnp.bfloat16),
-            pltpu.VMEM((PTS, WIN), jnp.bfloat16),
-            pltpu.VMEM((16, TB), jnp.float32),
+            pltpu.VMEM((PTS, PTS), jnp.bfloat16),
+            pltpu.VMEM((PTS, WIN), jnp.float32),
             pltpu.VMEM((16, TB), jnp.float32),
         ],
         compiler_params=pltpu.CompilerParams(vmem_limit_bytes=VMEM_LIMIT),
@@ -439,7 +460,7 @@
     )(total)
 
 
-def pieces_kernel(rec_ref, x_ref, parts_ref, out_ref, fields, phi_hi, phi_lo):
+def pieces_kernel(rec_ref, x_ref, parts_ref, out_ref, fields, spread, phi_hi, phi_lo):
     mb, mg = here()
     hi, lo, diag = own_pair(mb, mg)
 
@@ -460,7 +481,7 @@
         for r in range(2):
             block = mg + BLK * r
             fields[...] = rec_ref[r].T
-            build_phi(fields, (block * TB).astype(jnp.float32), lambda v, k: v, phi_hi, phi_lo)
+            build_phi(fields, block * TB, False, spread, phi_hi, phi_lo)
             for ref in (phi_hi, phi_lo):
                 ref[AUG:WIN, :] = jnp.zeros((WIN - AUG, PTS), jnp.bfloat16)
             gain = jnp.sum(parts_ref[r], axis=0)
@@ -493,6 +514,7 @@
         out_specs=vmem,
         scratch_shapes=[
             pltpu.VMEM((TB, TB), jnp.float32),
+            pltpu.VMEM((18, 16, TB), jnp.float32),
             pltpu.VMEM((WIN, PTS), jnp.bfloat16),
             pltpu.VMEM((WIN, PTS), jnp.bfloat16),
         ],
@@ -774,28 +796,58 @@
     )(tiles)
 
 
+STEP = 16
+
+
+def both(value):
+    return jnp.concatenate([value, value], axis=1)
+
+
 def eliminate(work):
-    for kb in range(TB // 8):
-        lo = 8 * kb
-        panel = work[lo : lo + 8, :]
-        row_at = lax.broadcasted_iota(jnp.int32, (8, 1), 0)
-        for j in range(8):
-            col = panel[:, lo + j : lo + j + 1]
-            pivot = panel[j : j + 1, :]
-            scale = lax.rsqrt(pivot[:, lo + j : lo + j + 1])
-            done = pivot * scale
-            panel = jnp.where(
-                row_at == j, done, panel - jnp.where(row_at > j, col * scale, 0.0) * done
-            )
-        work[lo : lo + 8, :] = panel
-        if lo + 8 < TB:
-            work[lo + 8 : TB, :] -= lax.dot_general(
-                panel[:, lo + 8 : TB],
-                panel,
-                (((0,), (0,)), ((), ())),
-                precision=EXACT,
-                preferred_element_type=jnp.float32,
-            )
+    at = lax.broadcasted_iota(jnp.int32, (8, WIN), 0)
+    for top in range(0, TB, STEP):
+        rows = [jnp.broadcast_to(work[top + i : top + i + 1, :], (8, WIN)) for i in range(STEP)]
+        entry = {
+            (i, j): jnp.broadcast_to(rows[i][:, top + j : top + j + 1], (8, TB))
+            for i in range(STEP)
+            for j in range(i + 1)
+        }
+        for j in range(STEP):
+            scale = lax.rsqrt(entry[j, j])
+            for i in range(j + 1, STEP):
+                entry[i, j] = entry[i, j] * scale
+            for i in range(j + 1, STEP):
+                for k in range(j + 1, i + 1):
+                    entry[i, k] = entry[i, k] - entry[i, j] * entry[k, j]
+            rows[j] = rows[j] * both(scale)
+            for i in range(j + 1, STEP):
+                rows[i] = rows[i] - both(entry[i, j]) * rows[j]
+        groups = []
+        for g in range(0, STEP, 8):
+            group = rows[g]
+            for i in range(1, 8):
+                group = jnp.where(at == i, rows[g + i], group)
+            groups.append(group)
+        panel = jnp.concatenate(groups, axis=0)
+        work[top : top + STEP, :] = panel
+        after = top + STEP
+        if after < TB:
+            high, low = split(panel)
+            left = jnp.concatenate([high, high, low], axis=0)
+            right = jnp.concatenate([high, low, high], axis=0)
+            for lo, up in ((after, after + STEP), (after + STEP, TB)):
+                if lo < up:
+                    work[lo:up, :] -= lax.dot_general(
+                        left[:, lo:up],
+                        right,
+                        (((0,), (0,)), ((), ())),
+                        preferred_element_type=jnp.float32,
+                    )
+
+
+def nt3(a, b):
+    (a_hi, a_lo), (b_hi, b_lo) = split(a), split(b)
+    return nt(a_hi, b_hi) + (nt(a_lo, b_hi) + nt(a_hi, b_lo))
 
 
 def factor_kernel(panel_ref, tile_ref, out_ref, work):
@@ -808,27 +860,12 @@
     eliminate(work)
     lower = jnp.where(row >= col, work[:, 0:TB].T, 0.0)
     inverse = jnp.where(row >= col, work[:, TB:WIN], 0.0)
-
-    def solve(n):
-        return lax.dot_general(
-            panel_ref[n],
-            inverse,
-            (((1,), (1,)), ((), ())),
-            precision=EXACT,
-            preferred_element_type=jnp.float32,
-        )
-
-    left = jnp.where(mg == 0, lower, solve(1))
+    solved = nt3(panel_ref[1:4].reshape(3 * TB, TB), inverse)
+    left = jnp.where(mg == 0, lower, solved[0:TB])
+    update = nt3(left, solved[TB : 3 * TB])
     for t in range(2):
         tile_col = mb + BLK * t
-        update = lax.dot_general(
-            left,
-            solve(2 + t),
-            (((1,), (1,)), ((), ())),
-            precision=EXACT,
-            preferred_element_type=jnp.float32,
-        )
-        value = jnp.where(tile_col == 0, left, tile_ref[t] - update)
+        value = jnp.where(tile_col == 0, left, tile_ref[t] - update[:, TB * t : TB * (t + 1)])
         keep = mg * TB + row >= tile_col * TB + col
         out_ref[0, :, t, :] = jnp.where(keep, value, 0.0)
 

time: 98.5 us -> 79.3 us (0.81)
  Pallas kernels: 95.8 us -> 76.5 us
    pallas_call x1, Pallas kernels: 16.9 us -> 6.07 us  [factor(): pl.pallas_call(factor_kernel, out_shape=jax.ShapeDtypeStruct((1, TB, 2, T...]
    pallas_call x1, Pallas kernels: 14.4 us -> 8.47 us  [pair_work(): pl.pallas_call(pair_kernel, out_shape=(jax.ShapeDtypeStruct((2, WIN, WIN)...]
    pallas_call x1, Pallas kernels: 13.3 us -> 10.8 us  [totals_exchange(): pl.pallas_call(totals_kernel, out_shape=jax.ShapeDtypeStruct((2, 16, 16,...]
where the time goes in v2:
time: 79.3 us; the launch traced here: 79.1 us
  Pallas kernels  76.5 us (96%)
  local copies, waits for them, and re-layouts  2.46 us (3%)
    pallas_call x1, Pallas kernels, share_panel(): pl.pallas_call(panel_kernel, out_shape=jax.ShapeDtypeStruct((4, TB, TB),...  27.5 us
    pallas_call x1, Pallas kernels, reduce_pieces(): pl.pallas_call(reduce_kernel, out_shape=jax.ShapeDtypeStruct((2, TB, TB),...  15.4 us
    pallas_call x1, Pallas kernels, totals_exchange(): pl.pallas_call(totals_kernel, out_shape=jax.ShapeDtypeStruct((2, 16, 16,...  10.8 us
    pallas_call x1, Pallas kernels, pair_work(): pl.pallas_call(pair_kernel, out_shape=(jax.ShapeDtypeStruct((2, WIN, WIN)...  8.47 us
    pallas_call x1, Pallas kernels, gather(): pl.pallas_call(gather_kernel, out_shape=jax.ShapeDtypeStruct((2, TB, TB),...  8.14 us
    pallas_call x1, Pallas kernels, factor(): pl.pallas_call(factor_kernel, out_shape=jax.ShapeDtypeStruct((1, TB, 2, T...  6.07 us
    unnamed x7, local copies, waits for them, and re-layouts  2.46 us

profile of v2, /device:TPU:127, one launch (start us, length us, event | category | flops | bytes accessed | tf_op | source)
XLA Modules:
  0.0 79.1 jit_solution(12378502628369670633)
XLA Ops:
  0.0 0.0 copy-start.2
  0.0 0.7 copy.5.points_ref
  0.7 0.0 copy-done.2
  0.7 0.0 copy-start
  0.7 0.9 %copy-done = f32[9,9,16]{2,1,0:T(8,128)S(1)} copy-done((f32[9,9,16]{2,1,0:T(8,128)S(1)}, f32[9,9,16]{2,1,0:T(8,128)}, u32[]{:S(2)}) %copy-start) | copy-done | bytes 5208
  1.6 0.0 copy-start.1
  1.6 0.8 %copy-done.1 = f32[128,128]{1,0:T(8,128)S(1)} copy-done((f32[128,128]{1,0:T(8,128)S(1)}, f32[128,128]{1,0:T(8,128)}, u32[]{:S(2)}) %copy-start.1) | copy-done | bytes 65560
  2.5 8.1 %gather_elements.1.rec_ref = f32[2,128,128]{2,1,0:T(8,128)S(1)} custom-call(f32[128,128]{1,0:T(8,128)S(1)} %copy-done.1, s32[16,9]{1,0:T(8,128)S(1)} %copy-done.2, f32[9,9,16]{2,1,0:T(8,128)S(1)} %copy-done, f32[3,9,16]{2,1,0:T(8,128)S(1)} %copy.5.points_ref), custom_call_target="tpu_custom_call" | custom-call | tf_op jit(solution)/shard_map/gather_elements/pallas_call | solution.py:193
  10.6 8.5 %pair_blocks.1 = (f32[2,256,256]{2,1,0:T(8,128)S(1)}, f32[2,16,128]{2,1,0:T(8,128)S(1)}) custom-call(f32[2,128,128]{2,1,0:T(8,128)S(1)} %gather_elements.1.rec_ref), custom_call_target="tpu_custom_call" | custom-call | tf_op jit(solution)/shard_map/pair_blocks/pallas_call | solution.py:364
  19.1 10.8 %send_totals.1.parts_ref = f32[2,16,16,128]{3,2,1,0:T(8,128)S(1)} custom-call(f32[2,16,128]{2,1,0:T(8,128)S(1)} %get-tuple-element.8.total_ref), custom_call_target="tpu_custom_call" | custom-call | tf_op jit(solution)/shard_map/send_totals/pallas_call | solution.py:450
  29.9 0.1 make_pieces.1.piece_ref
  30.1 15.4 %sum_pieces.1.tile_ref = f32[2,128,128]{2,1,0:T(8,128)S(1)} custom-call(f32[6,128,128]{2,1,0:T(8,128)S(1)} %make_pieces.1.piece_ref), custom_call_target="tpu_custom_call" | custom-call | tf_op jit(solution)/shard_map/sum_pieces/pallas_call | solution.py:636
  45.5 27.5 %share_panel.1.panel_ref = f32[4,128,128]{2,1,0:T(8,128)S(1)} custom-call(f32[2,128,128]{2,1,0:T(8,128)S(1)} %sum_pieces.1.tile_ref), custom_call_target="tpu_custom_call" | custom-call | tf_op jit(solution)/shard_map/share_panel/pallas_call | solution.py:786
  73.0 6.1 %factor_tiles.1 = f32[1,128,2,128]{3,2,1,0:T(2,128)} custom-call(f32[4,128,128]{2,1,0:T(8,128)S(1)} %share_panel.1.panel_ref, f32[2,128,128]{2,1,0:T(8,128)S(1)} %sum_pieces.1.tile_ref), custom_call_target="tpu_custom_call" | custom-call | tf_op jit(solution)/shard_map/factor_tiles/pallas_call | solution.py:875
Async XLA Ops:
  0.0 0.7 copy-start.2
  0.7 0.9 %copy-start = (f32[9,9,16]{2,1,0:T(8,128)S(1)}, f32[9,9,16]{2,1,0:T(8,128)}, u32[]{:S(2)}) copy-start(f32[9,9,16]{2,1,0:T(8,128)} %extract_ref.1) | copy-start | bytes 15556
  1.6 0.8 %copy-start.1 = (f32[128,128]{1,0:T(8,128)S(1)}, f32[128,128]{1,0:T(8,128)}, u32[]{:S(2)}) copy-start(f32[128,128]{1,0:T(8,128)} %constant.2.clone.map_ref) | copy-start | bytes 196612

commit v3 on v2

--- a/solution.py
+++ b/solution.py
@@ -186,26 +186,6 @@
         return carry
 
     lax.fori_loop(0, 16, finish, 0)
-
-
-def gather(conn, extract, points):
-    vmem = pl.BlockSpec(memory_space=pltpu.VMEM)
-    return pl.pallas_call(
-        gather_kernel,
-        out_shape=jax.ShapeDtypeStruct((2, TB, TB), jnp.float32),
-        in_specs=[vmem] * 4,
-        out_specs=vmem,
-        scratch_shapes=[
-            pltpu.VMEM((TB, TB), jnp.float32),
-            pltpu.VMEM((16, TB), jnp.float32),
-            pltpu.SemaphoreType.DMA((16,)),
-            pltpu.SemaphoreType.DMA((16,)),
-        ],
-        compiler_params=pltpu.CompilerParams(
-            collective_id=0, has_side_effects=True, vmem_limit_bytes=VMEM_LIMIT
-        ),
-        name="gather_elements",
-    )(jnp.asarray(field_map()), conn, extract, points)
 
 
 def split(value):
@@ -359,17 +339,29 @@
     lax.fori_loop(0, jnp.where(diag, 2, 1), run, 0)
 
 
-def pair_work(records):
+def gather_pair_kernel(
+    map_ref, conn_ref, extract_ref, points_ref, rec_ref, x_ref, total_ref, raw, record, send_sem, recv_sem, *rest
+):
+    gather_kernel(map_ref, conn_ref, extract_ref, points_ref, rec_ref, raw, record, send_sem, recv_sem)
+    pair_kernel(rec_ref, x_ref, total_ref, *rest)
+
+
+def gather_pair(conn, extract, points):
     vmem = pl.BlockSpec(memory_space=pltpu.VMEM)
     return pl.pallas_call(
-        pair_kernel,
+        gather_pair_kernel,
         out_shape=(
+            jax.ShapeDtypeStruct((2, TB, TB), jnp.float32),
             jax.ShapeDtypeStruct((2, WIN, WIN), jnp.float32),
             jax.ShapeDtypeStruct((2, 16, TB), jnp.float32),
         ),
-        in_specs=[vmem],
-        out_specs=(vmem, vmem),
+        in_specs=[vmem] * 4,
+        out_specs=(vmem, vmem, vmem),
         scratch_shapes=[
+            pltpu.VMEM((TB, TB), jnp.float32),
+            pltpu.VMEM((16, TB), jnp.float32),
+            pltpu.SemaphoreType.DMA((16,)),
+            pltpu.SemaphoreType.DMA((16,)),
             pltpu.VMEM((2, TB, TB), jnp.float32),
             pltpu.VMEM((18, 16, TB), jnp.float32),
             pltpu.VMEM((2, WIN, PTS), jnp.bfloat16),
@@ -381,9 +373,11 @@
             pltpu.VMEM((PTS, WIN), jnp.float32),
             pltpu.VMEM((16, TB), jnp.float32),
         ],
-        compiler_params=pltpu.CompilerParams(vmem_limit_bytes=VMEM_LIMIT),
-        name="pair_blocks",
-    )(records)
+        compiler_params=pltpu.CompilerParams(
+            collective_id=0, has_side_effects=True, vmem_limit_bytes=VMEM_LIMIT
+        ),
+        name="gather_and_pair",
+    )(jnp.asarray(field_map()), conn, extract, points)
 
 
 def totals_kernel(total_ref, out_ref, send_sem, recv_sem):
@@ -884,8 +878,7 @@
 
 
 def shards(conn, extract, points):
-    records = gather(conn, extract, points)
-    x, total = pair_work(records)
+    records, x, total = gather_pair(conn, extract, points)
     parts = totals_exchange(total)
     pieces = make_pieces(records, x, parts)
     tiles = reduce_pieces(pieces)

time: 79.3 us -> 79.3 us (level)
    pallas_call x2 -> x1, Pallas kernels: 16.6 us -> 16.6 us  [gather_pair(): pl.pallas_call(gather_pair_kernel, out_shape=(jax.ShapeDtypeStruct((2, TB...]
where the time goes in v3:
time: 79.3 us; the launch traced here: 79.1 us
  Pallas kernels  76.6 us (97%)
  local copies, waits for them, and re-layouts  2.46 us (3%)
    pallas_call x1, Pallas kernels, share_panel(): pl.pallas_call(panel_kernel, out_shape=jax.ShapeDtypeStruct((4, TB, TB),...  27.5 us
    pallas_call x1, Pallas kernels, gather_pair(): pl.pallas_call(gather_pair_kernel, out_shape=(jax.ShapeDtypeStruct((2, TB...  16.6 us
    pallas_call x1, Pallas kernels, reduce_pieces(): pl.pallas_call(reduce_kernel, out_shape=jax.ShapeDtypeStruct((2, TB, TB),...  15.4 us
    pallas_call x1, Pallas kernels, totals_exchange(): pl.pallas_call(totals_kernel, out_shape=jax.ShapeDtypeStruct((2, 16, 16,...  10.8 us
    pallas_call x1, Pallas kernels, factor(): pl.pallas_call(factor_kernel, out_shape=jax.ShapeDtypeStruct((1, TB, 2, T...  6.08 us
    unnamed x7, local copies, waits for them, and re-layouts  2.46 us

profile of v3, /device:TPU:127, one launch (start us, length us, event | category | flops | bytes accessed | tf_op | source)
XLA Modules:
  0.0 79.1 jit_solution(7516977177438812816)
XLA Ops:
  0.0 0.0 copy-start.2
  0.0 0.7 copy.5.points_ref
  0.7 0.0 copy-done.2
  0.7 0.0 copy-start
  0.7 0.9 %copy-done = f32[9,9,16]{2,1,0:T(8,128)S(1)} copy-done((f32[9,9,16]{2,1,0:T(8,128)S(1)}, f32[9,9,16]{2,1,0:T(8,128)}, u32[]{:S(2)}) %copy-start) | copy-done | bytes 5208
  1.6 0.0 copy-start.1
  1.6 0.8 %copy-done.1 = f32[128,128]{1,0:T(8,128)S(1)} copy-done((f32[128,128]{1,0:T(8,128)S(1)}, f32[128,128]{1,0:T(8,128)}, u32[]{:S(2)}) %copy-start.1) | copy-done | bytes 65560
  2.5 16.6 %gather_and_pair.1 = (f32[2,128,128]{2,1,0:T(8,128)S(1)}, f32[2,256,256]{2,1,0:T(8,128)S(1)}, f32[2,16,128]{2,1,0:T(8,128)S(1)}) custom-call(f32[128,128]{1,0:T(8,128)S(1)} %copy-done.1, s32[16,9]{1,0:T(8,128)S(1)} %copy-done.2, f32[9,9,16]{2,1,0:T(8,128)S(1)} %copy-done, f32[3,9,16]{2,1,0:T(8,128)S(1)} %copy.5.points_ref), custom_call_target="tpu_custom_call" | custom-call | tf_op jit(solution)/shard_map/gather_and_pair/pallas_call | solution.py:351
  19.1 10.8 %send_totals.1.parts_ref = f32[2,16,16,128]{3,2,1,0:T(8,128)S(1)} custom-call(f32[2,16,128]{2,1,0:T(8,128)S(1)} %get-tuple-element.10.total_ref), custom_call_target="tpu_custom_call" | custom-call | tf_op jit(solution)/shard_map/send_totals/pallas_call | solution.py:444
  29.9 0.1 make_pieces.1.piece_ref
  30.1 15.4 %sum_pieces.1.tile_ref = f32[2,128,128]{2,1,0:T(8,128)S(1)} custom-call(f32[6,128,128]{2,1,0:T(8,128)S(1)} %make_pieces.1.piece_ref), custom_call_target="tpu_custom_call" | custom-call | tf_op jit(solution)/shard_map/sum_pieces/pallas_call | solution.py:630
  45.5 27.5 %share_panel.1.panel_ref = f32[4,128,128]{2,1,0:T(8,128)S(1)} custom-call(f32[2,128,128]{2,1,0:T(8,128)S(1)} %sum_pieces.1.tile_ref), custom_call_target="tpu_custom_call" | custom-call | tf_op jit(solution)/shard_map/share_panel/pallas_call | solution.py:780
  73.0 6.1 %factor_tiles.1 = f32[1,128,2,128]{3,2,1,0:T(2,128)} custom-call(f32[4,128,128]{2,1,0:T(8,128)S(1)} %share_panel.1.panel_ref, f32[2,128,128]{2,1,0:T(8,128)S(1)} %sum_pieces.1.tile_ref), custom_call_target="tpu_custom_call" | custom-call | tf_op jit(solution)/shard_map/factor_tiles/pallas_call | solution.py:869
Async XLA Ops:
  0.0 0.7 copy-start.2
  0.7 0.9 %copy-start = (f32[9,9,16]{2,1,0:T(8,128)S(1)}, f32[9,9,16]{2,1,0:T(8,128)}, u32[]{:S(2)}) copy-start(f32[9,9,16]{2,1,0:T(8,128)} %extract_ref.1) | copy-start | bytes 15556
  1.6 0.8 %copy-start.1 = (f32[128,128]{1,0:T(8,128)S(1)}, f32[128,128]{1,0:T(8,128)}, u32[]{:S(2)}) copy-start(f32[128,128]{1,0:T(8,128)} %constant.2.clone.map_ref) | copy-start | bytes 196612

commit v4 on v0

v4 whole, which is shorter than its diff:
```python
import functools
import math

import jax
import jax.numpy as jnp
import numpy as np
from jax import lax
from jax.experimental import pallas as pl
from jax.experimental.pallas import tpu as pltpu
from jax.sharding import PartitionSpec as P

M = 2048
EX = 64
EY = 32
QP = 9
TB = 128
BLK = 8
GRID = 16
PTS = QP * TB
WIN = 256
AUG = 192

KERNEL_GAIN = 0.02
MASS_SHIFT = 0.05

FX, FY, FW, FV, FC = 0, 9, 18, 27, 108

MESH = pl.DeviceIdType.MESH
VMEM_LIMIT = 48 * 1024 * 1024
EXACT = lax.Precision.HIGHEST


def bernstein_table():
    spread_root = 0.5 * math.sqrt(0.6)
    nodes = [0.5 - spread_root, 0.5, 0.5 + spread_root]
    poly = [[(1.0 - t) ** 2, 2.0 * t * (1.0 - t), t * t] for t in nodes]
    return np.array(
        [
            [poly[i][a] * poly[j][b] for a in range(3) for b in range(3)]
            for i in range(3)
            for j in range(3)
        ],
        np.float32,
    )


def bernstein_lanes():
    table = np.zeros((16, TB), np.float32)
    table[:QP, :QP] = bernstein_table()
    return table


def column_device(column, place):
    return column // 2, 8 * (column % 2) + place


def differs(b, g, mb, mg):
    return jnp.logical_or(b != mb, g != mg)


def remote(src, dst, send_sem, recv_sem, b, g):
    return pltpu.make_async_remote_copy(
        src_ref=src,
        dst_ref=dst,
        send_sem=send_sem,
        recv_sem=recv_sem,
        device_id=(b, g),
        device_id_type=MESH,
    )


def others(b, g):
    return [(b, (g + n) % GRID) for n in range(1, GRID)] + [((b + n) % BLK, g) for n in range(1, BLK)]


def when(condition):
    return pl.when(condition)


def split(value):
    high = value.astype(jnp.bfloat16)
    return high, (value - high.astype(jnp.float32)).astype(jnp.bfloat16)


def build_phi(fields, start, weigh, spread, high_ref, low_ref):
    lane = lax.broadcasted_iota(jnp.int32, (QP, TB), 1)
    cell_y = lane % EY
    cell_x = lane // EY
    target = fields[FC : FC + QP, :].astype(jnp.int32) - start
    target = jnp.where(target < 0, target + M, target)
    place = 3 * (target // EY - cell_x) + (target % EY - cell_y + EY) % EY
    weight = fields[FW : FW + QP, :]
    slots = [jnp.zeros((QP, TB), jnp.float32) for _ in range(QP)]
    for a in range(QP):
        value = fields[FV + QP * a : FV + QP * (a + 1), :]
        if weigh:
            value = value * weight
        here_a = jnp.broadcast_to(place[a : a + 1, :], (QP, TB))
        for n in range(QP):
            slots[n] = jnp.where(here_a == n, value, slots[n])
    for jx in range(6):
        for t in range(3):
            row = jnp.zeros((QP, TB), jnp.float32)
            for step in range(3):
                if 0 <= jx - step <= 3:
                    row = jnp.where(cell_x == jx - step, slots[3 * step + t], row)
            spread[3 * jx + t, 0:QP, :] = row
    rows = EY
    wide_y = lax.broadcasted_iota(jnp.int32, (rows, TB), 1) % EY
    down_y = lax.broadcasted_iota(jnp.int32, (rows, TB), 0)
    hits = [(wide_y + t) % EY == down_y for t in range(3)]
    for jx in range(6):
        for k in range(QP):
            value = jnp.zeros((rows, TB), jnp.float32)
            for t in range(3):
                line = jnp.broadcast_to(spread[3 * jx + t, k : k + 1, :], (rows, TB))
                value = jnp.where(hits[t], line, value)
            high, low = split(value)
            high_ref[rows * jx : rows * (jx + 1), TB * k : TB * (k + 1)] = high
            low_ref[rows * jx : rows * (jx + 1), TB * k : TB * (k + 1)] = low


def nt(a, b):
    return lax.dot_general(a, b, (((1,), (1,)), ((), ())), preferred_element_type=jnp.float32)


def nn(a, b):
    return lax.dot_general(a, b, (((1,), (0,)), ((), ())), preferred_element_type=jnp.float32)


STEP = 16


def both(value):
    return jnp.concatenate([value, value], axis=1)


def eliminate(work):
    at = lax.broadcasted_iota(jnp.int32, (8, WIN), 0)
    for top in range(0, TB, STEP):
        rows = [jnp.broadcast_to(work[top + i : top + i + 1, :], (8, WIN)) for i in range(STEP)]
        entry = {
            (i, j): jnp.broadcast_to(rows[i][:, top + j : top + j + 1], (8, TB))
            for i in range(STEP)
            for j in range(i + 1)
        }
        for j in range(STEP):
            scale = lax.rsqrt(entry[j, j])
            for i in range(j + 1, STEP):
                entry[i, j] = entry[i, j] * scale
            for i in range(j + 1, STEP):
                for k in range(j + 1, i + 1):
                    entry[i, k] = entry[i, k] - entry[i, j] * entry[k, j]
            rows[j] = rows[j] * both(scale)
            for i in range(j + 1, STEP):
                rows[i] = rows[i] - both(entry[i, j]) * rows[j]
        groups = []
        for g in range(0, STEP, 8):
            group = rows[g]
            for i in range(1, 8):
                group = jnp.where(at == i, rows[g + i], group)
            groups.append(group)
        panel = jnp.concatenate(groups, axis=0)
        work[top : top + STEP, :] = panel
        after = top + STEP
        if after < TB:
            high, low = split(panel)
            left = jnp.concatenate([high, high, low], axis=0)
            right = jnp.concatenate([high, low, high], axis=0)
            for lo, up in ((after, after + STEP), (after + STEP, TB)):
                if lo < up:
                    work[lo:up, :] -= lax.dot_general(
                        left[:, lo:up],
                        right,
                        (((0,), (0,)), ((), ())),
                        preferred_element_type=jnp.float32,
                    )


def nt3(a, b):
    (a_hi, a_lo), (b_hi, b_lo) = split(a), split(b)
    return nt(a_hi, b_hi) + (nt(a_lo, b_hi) + nt(a_hi, b_lo))


HALF_X = float(EX) / 4.0
HALF_Y = float(EY) / 4.0


def make_record(bern, conn, extract, points, raw):
    raw[...] = jnp.zeros_like(raw)
    for c in range(3):
        raw[QP * c : QP * (c + 1), 0:16] = points[:, c, :]
    for a in range(QP):
        value = jnp.zeros((QP, 16), jnp.float32)
        for n in range(QP):
            value = value + bern[0:QP, n : n + 1] * extract[a, n : n + 1, :]
        raw[FV + QP * a : FV + QP * (a + 1), 0:16] = value
    raw[FC : FC + QP, 0:16] = conn[...].astype(jnp.float32).T
    return raw[...].T[0:16, :]


def set_up_block(slot, block, shift, rec, fields, spread, phi_hi, phi_lo, trial_x, trial_y):
    cell_y = lax.broadcasted_iota(jnp.int32, (QP, TB), 1) % EY
    first = lax.broadcasted_iota(jnp.int32, (16, TB), 0) == 0
    view = fields.at[slot]
    view[...] = rec[slot].T
    build_phi(view, block * TB, True, spread, phi_hi.at[slot], phi_lo.at[slot])
    for ref in (phi_hi, phi_lo):
        ref[slot, AUG:WIN, :] = jnp.zeros((WIN - AUG, PTS), jnp.bfloat16)
    for k in range(QP):
        weight = jnp.broadcast_to(view[FW + k : FW + k + 1, :], (16, TB))
        high, low = split(jnp.where(first, weight, 0.0))
        phi_hi[slot, AUG : AUG + 16, TB * k : TB * (k + 1)] = high
        phi_lo[slot, AUG : AUG + 16, TB * k : TB * (k + 1)] = low
    trial_x[slot, 0:QP, :] = view[FX : FX + QP, :] * (EX / 2.0) + shift
    for quarter in range(4):
        turn = jnp.where(cell_y > 8 * quarter + 8, -HALF_Y, HALF_Y)
        trial_y[slot, quarter, 0:QP, :] = view[FY : FY + QP, :] * (EX / 2.0) + turn


def kernel_chunk(i, j, q_slot, trial_x, trial_y, splat, kern):
    qx = jnp.broadcast_to(trial_x[q_slot, pl.ds(j, 1), :], (8, TB))
    qy = [jnp.broadcast_to(trial_y[q_slot, quarter, pl.ds(j, 1), :], (8, TB)) for quarter in range(4)]
    sums = jnp.zeros((8, TB), jnp.float32)
    for h in range(8):
        values = []
        for n in (2 * h, 2 * h + 1):
            rows = slice(8 * n, 8 * n + 8)
            gap_x = HALF_X - jnp.abs(qx - splat[0, rows, :])
            gap_y = HALF_Y - jnp.abs(splat[1, rows, :] - qy[n % 4])
            root = lax.rsqrt(1.0 + (gap_x * gap_x + gap_y * gap_y))
            square = root * root
            value = square * square * lax.rsqrt(root)
            sums = sums + value * splat[2, rows, :]
            values.append(value)
        kern[TB * i + 16 * h : TB * i + 16 * h + 16, pl.ds(pl.multiple_of(j * TB, TB), TB)] = (
            jnp.concatenate(values, axis=0).astype(jnp.bfloat16)
        )
    return jnp.sum(sums, axis=0, keepdims=True)


def below(value):
    return jnp.concatenate([value, jnp.zeros((TB - 64, TB), jnp.float32)], axis=0)


def stiffness_kernel(
    bern_in, conn_in, extract_in, points_in, out_ref,
    bern, conn, extract, points, raw, rec, fields, spread, phi_hi, phi_lo, trial_x, trial_y, splat, kern, pot,
    col_sum, totals, parts, xs, stage_big, stage_small, land_big, land_small, tiles, head, row_tile, col_tile, work,
    in_sem, rec_send, rec_recv, total_send, total_recv, piece_send, big_recv, small_recv,
    head_send, head_recv, row_send, row_recv, col_send, col_recv, ready,
):
    mb, mg = lax.axis_index("blk"), lax.axis_index("grid")
    own = 2 * mb + mg // 8
    place = mg % 8
    core = mg % 2
    chip = mg // 2
    last = place == 7
    partner = mg + 1 - 2 * core
    barrier = pltpu.get_barrier_semaphore()

    fetch = [
        pltpu.make_async_copy(src, dst, in_sem.at[n])
        for n, (src, dst) in enumerate(
            ((bern_in, bern), (extract_in, extract), (points_in, points), (conn_in, conn))
        )
    ]
    for copy in fetch:
        copy.start()
    row_tile[...] = jnp.zeros_like(row_tile)
    col_tile[...] = jnp.zeros_like(col_tile)
    for b, g in others(mb, mg):
        pl.semaphore_signal(barrier, inc=1, device_id=(b, g), device_id_type=MESH)
    for copy in fetch:
        copy.wait()
    mine = pl.ds(pl.multiple_of(16 * place, 16), 16)
    rec[0, mine, :] = make_record(bern, conn, extract, points, raw)
    pl.semaphore_wait(barrier, GRID - 1 + BLK - 1)
    for n in range(1, BLK):
        pl.semaphore_signal(ready, inc=1, device_id=((mb + n) % BLK, mg), device_id_type=MESH)

    base = 8 * (mg // 8)
    z = place // 2

    def record_copy(from_z, from_core, n, g):
        at = 2 * from_z + from_core
        view = rec.at[0, pl.ds(16 * at, 16), :]
        return remote(view, view, rec_send.at[n], rec_recv.at[at], mb, g)

    record_copy(z, core, 0, partner).start()
    for n in range(1, 4):
        record_copy(z, core, n, base + 2 * ((z + n) % 4) + core).start()
    for n in range(1, 4):
        from_z = (z + 4 - n) % 4
        record_copy(from_z, core, 0, mg).wait_recv()
        record_copy(from_z, core, 3 + n, partner).start()
    for n in range(4):
        record_copy((z + 4 - n) % 4, 1 - core, 0, mg).wait_recv()
    pl.semaphore_wait(ready, BLK - 1)
    to_b, to_g = column_device((own + 15 - place) % 16, place)
    block_copy = remote(rec.at[0], rec.at[1], rec_send.at[7], rec_recv.at[8], to_b, to_g)
    block_copy.start()

    other = (own + 1 + place) % 16
    set_up_block(0, own, -HALF_X, rec, fields, spread, phi_hi, phi_lo, trial_x, trial_y)
    block_copy.wait_recv()
    wrapped = jnp.where(other < own, HALF_X, -HALF_X)
    set_up_block(1, other, wrapped, rec, fields, spread, phi_hi, phi_lo, trial_x, trial_y)

    lower = own < 8

    def evaluate(i, low, high, q_slot):
        def part(j, carry):
            col_sum[pl.ds(j, 1), :] += kernel_chunk(i, j, q_slot, trial_x, trial_y, splat, kern)
            return carry

        steps = high - low
        lax.fori_loop(low, high, part, 0, unroll=3 if steps % 3 == 0 else 2 if steps % 2 == 0 else 1)

    def run(r):
        q_slot = 1 - r
        col_sum[...] = jnp.zeros_like(col_sum)
        if r == 0:
            @when(jnp.logical_and(last, lower))
            def _():
                kern[5 * TB : PTS, :] = jnp.zeros((4 * TB, PTS), jnp.bfloat16)

            @when(jnp.logical_and(last, jnp.logical_not(lower)))
            def _():
                kern[:, 0 : 5 * TB] = jnp.zeros((PTS, 5 * TB), jnp.bfloat16)

        for i in range(QP):
            for n, field in ((0, FX), (1, FY), (2, FW)):
                picked = rec[0, :, field + i : field + i + 1] * (EX / 2.0 if n < 2 else KERNEL_GAIN)
                splat[n] = jnp.broadcast_to(picked, (TB, TB))
            if r == 1:
                at = slice(TB * i, TB * (i + 1))
                if i > 0:
                    kern[at, 0 : TB * i] = jnp.zeros((TB, TB * i), jnp.bfloat16)
                col_sum[i : i + 1, :] += 0.5 * kernel_chunk(i, i, q_slot, trial_x, trial_y, splat, kern)
                kern[at, at] = kern[at, at] * 0.5
                if i + 1 < QP:
                    evaluate(i, i + 1, QP, q_slot)
                continue
            whole = jnp.logical_not(last)
            if i < 5:
                whole = jnp.logical_or(whole, lower)

            @when(whole)
            def _(i=i):
                evaluate(i, 0, QP, q_slot)

            @when(jnp.logical_and(last, jnp.logical_not(lower)))
            def _(i=i):
                evaluate(i, 5, QP, q_slot)

        pot[...] = nt(kern[...], phi_hi[q_slot]) + nt(kern[...], phi_lo[q_slot])

        columns = [
            pot[TB * i : TB * (i + 1), TB:WIN].T[AUG - TB : AUG - TB + 1, :] * KERNEL_GAIN for i in range(QP)
        ]
        if r == 0:
            totals[1, 0:QP, :] = col_sum[0:QP, :]
            for i in range(QP):
                totals[0, i : i + 1, :] = columns[i]
            total_copy(1).start()

            @when(jnp.logical_not(last))
            def _():
                total_copy(0).start()
        else:
            for i in range(QP):
                parts[7, i : i + 1, :] = totals[0, i : i + 1, :] + col_sum[i : i + 1, :] + columns[i]

        high, low = split(pot[...])
        inside = jnp.logical_and(
            lax.broadcasted_iota(jnp.int32, (WIN, WIN), 0) < AUG,
            lax.broadcasted_iota(jnp.int32, (WIN, WIN), 1) < AUG,
        )
        value = nn(phi_hi[0], high) + nn(phi_lo[0], high) + nn(phi_hi[0], low)
        xs[...] = jnp.where(inside, -KERNEL_GAIN * value, 0.0)
        if r == 0:
            pair_pieces()

    def total_copy(n):
        b, g = column_device(other if n == 1 else own, 7)
        slot = 8 + place if n == 1 else place
        return remote(totals.at[n], parts.at[slot], total_send.at[n], total_recv.at[slot], b, g)

    def target(n):
        if n < 4:
            u, v = (0, 1, 0, 1)[n], (0, 0, 1, 1)[n]
            row, col = (own + u) % 16, (other + v) % 16
            slot = {0: 0, 1: jnp.where(row < col, 1, 2), 2: jnp.where(row < col, 2, 1), 3: 3}[n]
            half = jnp.where(jnp.logical_and(last, own >= 8), 1, 0)
        else:
            after = (own + 1) % 16
            row, col = (own, after, after)[n - 4], (own, own, after)[n - 4]
            slot = {4: 0, 5: jnp.where(own == 15, 1, 2), 6: 3}[n]
            half = 0
        big, small = jnp.maximum(row, col), jnp.minimum(row, col)
        return small % BLK, big, small // BLK, slot, half, row < col

    STAGE = {0: 0, 4: 1, 1: 0, 2: 1, 3: 2, 5: 3, 6: 4}

    def piece_copy(n):
        b, g, t, slot, half, flip = target(n)
        if n in (0, 4):
            return stage_big.at[STAGE[n]], land_big.at[t, half], big_recv.at[t, half], b, g
        return stage_small.at[STAGE[n]], land_small.at[t, slot - 1, half], small_recv.at[t, slot - 1, half], b, g

    def send_piece(n):
        src, dst, sem, b, g = piece_copy(n)

        @when(differs(b, g, mb, mg))
        def _():
            remote(src, dst, piece_send.at[n], sem, b, g).start()

        @when(jnp.logical_not(differs(b, g, mb, mg)))
        def _():
            pltpu.make_async_copy(src, dst, piece_send.at[n]).start()

    def drain_piece(n):
        src, dst, sem, b, g = piece_copy(n)

        @when(differs(b, g, mb, mg))
        def _():
            remote(src, dst, piece_send.at[n], sem, b, g).wait_send()

    def settle_piece(n):
        src, dst, sem, b, g = piece_copy(n)

        @when(jnp.logical_not(differs(b, g, mb, mg)))
        def _():
            pltpu.make_async_copy(src, dst, piece_send.at[n]).wait()

    def pair_pieces():
        corner, side = slice(0, TB), slice(TB, TB + 64)
        flip0 = target(0)[5]
        flip3 = target(3)[5]

        @when(flip0)
        def _():
            stage_big[0] = xs[corner, corner].T

        @when(jnp.logical_not(flip0))
        def _():
            stage_big[0] = xs[corner, corner]

        send_piece(0)
        stage_small[0] = xs[side, corner]
        send_piece(1)
        stage_small[1] = xs[corner, TB:WIN].T[0:64, :]
        send_piece(2)

        @when(flip3)
        def _():
            stage_small[2] = xs[TB:WIN, TB:WIN].T[0:64, :]

        @when(jnp.logical_not(flip3))
        def _():
            stage_small[2] = xs[side, TB:WIN]

        send_piece(3)

    run(0)

    @when(last)
    def _():
        run(1)
        build_phi(fields.at[0], own * TB, False, spread, phi_hi.at[1], phi_lo.at[1])
        for ref in (phi_hi, phi_lo):
            ref[1, AUG:WIN, :] = jnp.zeros((WIN - AUG, PTS), jnp.bfloat16)
        for n in range(16):
            if n != 7:
                remote(totals.at[0], parts.at[n], total_send.at[0], total_recv.at[n], mb, mg).wait_recv()
        gain = parts[0]
        for n in range(1, 16):
            gain = gain + parts[n]
        mass = xs[...] + xs[...].T
        for k in range(QP):
            lanes = slice(TB * k, TB * (k + 1))
            left = phi_hi[1, :, lanes].astype(jnp.float32) + phi_lo[1, :, lanes].astype(jnp.float32)
            factor = fields[0, FW + k : FW + k + 1, :] * (MASS_SHIFT + gain[k : k + 1, :])
            high, low = split(left * factor)
            mass += nt(high, phi_hi[1, :, lanes]) + nt(low, phi_hi[1, :, lanes]) + nt(high, phi_lo[1, :, lanes])
        stage_big[1] = mass[0:TB, 0:TB]
        send_piece(4)
        stage_small[3] = mass[TB : TB + 64, 0:TB]
        send_piece(5)
        stage_small[4] = mass[TB : TB + 64, TB:WIN]
        send_piece(6)

    for n in range(4):
        settle_piece(n)

    @when(last)
    def _():
        for n in range(4, 7):
            settle_piece(n)

    for t in range(2):
        tile_col = mb + BLK * t
        owned = mg >= tile_col
        square = mg == tile_col
        tiles[t] = jnp.zeros((TB, TB), jnp.float32)
        for slot in range(4):
            first, second = (mg - slot // 2 + 16) % 16, (tile_col - slot % 2 + 16) % 16
            ahead = (first - second + 16) % 16
            skip = jnp.logical_and(square, slot == 1)
            for half in range(2):
                host = jnp.where(ahead < 8, second, first)
                step = jnp.where(ahead == 0, 7, jnp.where(ahead < 8, ahead - 1, 15 - ahead))
                if half == 0:
                    host = jnp.where(ahead == 8, jnp.minimum(first, second), host)
                    there = jnp.logical_and(owned, jnp.logical_not(skip))
                else:
                    host = jnp.maximum(first, second)
                    there = jnp.logical_and(owned, ahead == 8)
                from_b, from_g = column_device(host, step)
                if slot == 0:
                    src, dst, sem = stage_big.at[0], land_big.at[t, half], big_recv.at[t, half]
                else:
                    src = stage_small.at[0]
                    dst, sem = land_small.at[t, slot - 1, half], small_recv.at[t, slot - 1, half]

                @when(there)
                def _(src=src, dst=dst, sem=sem, t=t, slot=slot, square=square, from_b=from_b, from_g=from_g):
                    @when(differs(from_b, from_g, mb, mg))
                    def _():
                        remote(src, dst, piece_send.at[0], sem, mb, mg).wait_recv()

                    if slot == 0:
                        tiles[t] += dst[...]
                    elif slot == 1:
                        tiles[t] += below(dst[...]).T
                    elif slot == 3:
                        tiles[t, 0:64, :] += dst[...]
                    else:
                        tiles[t, 0:64, :] += dst[...]

                        @when(square)
                        def _():
                            tiles[t] += below(dst[...]).T

    first = mb == 0
    upper_half = core == 0
    half_rows = pl.ds(pl.multiple_of(64 * core, 64), 64)
    other_rows = pl.ds(pl.multiple_of(64 * (1 - core), 64), 64)
    active = mb <= 2 * chip + 1
    relay = jnp.logical_and(mg >= 1, mb == mg % BLK)
    special = jnp.logical_and(first, mg % BLK != 0)

    def row_copy(n, b):
        return remote(tiles.at[0], row_tile, row_send.at[n], row_recv, b, mg)

    @when(special)
    def _():
        row_copy(0, mg % BLK).start()

    def head_half(n, b, g, rows):
        return remote(head.at[rows, :], head.at[rows, :], head_send.at[n], head_recv.at[0], b, g)

    def head_swap(rows, g):
        return remote(head.at[rows, :], head.at[rows, :], head_send.at[15], head_recv.at[1], mb, g)

    root = jnp.logical_and(first, mg == 0)
    root_pair = jnp.logical_and(first, chip == 0)
    whole_head = remote(head, head, head_send.at[16], head_recv.at[2], mb, partner)

    @when(root)
    def _():
        head[...] = tiles[0]
        whole_head.start()

    @when(jnp.logical_and(root_pair, mg == 1))
    def _():
        whole_head.wait_recv()

    @when(root_pair)
    def _():
        for n in range(1, 8):
            head_half(n, 0, 2 * n + core, half_rows).start()

    @when(jnp.logical_and(first, mg == 8))
    def _():
        row_tile[...] = tiles[0]

    def relay_copy(n):
        return remote(row_tile, col_tile.at[mg // BLK], col_send.at[n], col_recv.at[mg // BLK], mb, 2 * n + core)

    relay_partner = remote(
        row_tile, col_tile.at[mg // BLK], col_send.at[8], col_recv.at[mg // BLK], mb, partner
    )
    with_partner = jnp.logical_and(relay, core == 0)

    @when(jnp.logical_and(relay, jnp.logical_not(first)))
    def _():
        row_copy(0, mb).wait_recv()

    for n in range(1, 8):
        @when(jnp.logical_and(relay, chip < n))
        def _(n=n):
            relay_copy(n).start()

    @when(with_partner)
    def _():
        relay_partner.start()

    @when(jnp.logical_and(active, jnp.logical_not(root_pair)))
    def _():
        head_half(0, mb, mg, half_rows).wait_recv()

    for n in range(1, 8):
        @when(jnp.logical_and(first, n <= 2 * chip + 1))
        def _(n=n):
            head_half(7 + n, n, mg, half_rows).start()

    swaps = jnp.logical_and(active, jnp.logical_not(root_pair))

    @when(swaps)
    def _():
        head_swap(half_rows, partner).start()

    for n in range(1, 8):
        @when(jnp.logical_and(first, jnp.logical_and(n <= mg, n != mg % BLK)))
        def _(n=n):
            row_copy(n, n).start()

    @when(swaps)
    def _():
        head_swap(other_rows, partner).wait_recv()

    def forward(t):
        return remote(col_tile.at[t], col_tile.at[t], col_send.at[9 + t], col_recv.at[t], mb, partner)

    for t in range(2):
        tile_col = mb + BLK * t
        wants = jnp.logical_and(tile_col >= 1, mg > tile_col)

        @when(wants)
        def _(t=t, tile_col=tile_col):
            forward(t).wait_recv()

            @when(core == tile_col % 2)
            def _():
                forward(t).start()

    needs_row = jnp.logical_and(jnp.logical_not(first), jnp.logical_and(mb <= mg, jnp.logical_not(relay)))

    row = lax.broadcasted_iota(jnp.int32, (TB, TB), 0)
    col = lax.broadcasted_iota(jnp.int32, (TB, TB), 1)
    busy = mg >= mb

    @when(busy)
    def _():
        work[:, 0:TB] = 0.5 * (head[...] + head[...].T)
        work[:, TB:WIN] = jnp.where(row == col, 1.0, 0.0)
        eliminate(work)

        @when(needs_row)
        def _():
            row_copy(0, mb).wait_recv()

        lower = jnp.where(row >= col, work[:, 0:TB].T, 0.0)
        inverse = jnp.where(row >= col, work[:, TB:WIN], 0.0)
        row_value = jnp.where(first, tiles[0], row_tile[...])
        columns = [jnp.where(mg == mb + BLK * t, row_value, col_tile[t]) for t in range(2)]
        solved = nt3(jnp.concatenate([row_value] + columns, axis=0), inverse)
        left = jnp.where(mg == 0, lower, solved[0:TB])
        update = nt3(left, solved[TB : 3 * TB])
        for t in range(2):
            tile_col = mb + BLK * t
            value = jnp.where(tile_col == 0, left, tiles[t] - update[:, TB * t : TB * (t + 1)])
            keep = mg * TB + row >= tile_col * TB + col
            out_ref[0, :, t, :] = jnp.where(keep, value, 0.0)

    @when(jnp.logical_not(busy))
    def _():
        out_ref[...] = jnp.zeros_like(out_ref)

    record_copy(z, core, 0, partner).wait_send()
    for n in range(1, 4):
        record_copy(z, core, n, partner).wait_send()
        record_copy(z, core, 3 + n, partner).wait_send()
    block_copy.wait_send()
    total_copy(1).wait_send()

    @when(jnp.logical_not(last))
    def _():
        total_copy(0).wait_send()

    for n in range(4):
        drain_piece(n)

    @when(last)
    def _():
        for n in range(4, 7):
            drain_piece(n)

    @when(special)
    def _():
        row_copy(0, mg % BLK).wait_send()

    @when(root)
    def _():
        whole_head.wait_send()

    @when(root_pair)
    def _():
        for n in range(1, 8):
            head_half(n, 0, mg, half_rows).wait_send()

    @when(swaps)
    def _():
        head_swap(half_rows, partner).wait_send()

    for n in range(1, 8):
        @when(jnp.logical_and(relay, chip < n))
        def _(n=n):
            relay_copy(n).wait_send()

        @when(jnp.logical_and(first, n <= 2 * chip + 1))
        def _(n=n):
            head_half(7 + n, n, mg, half_rows).wait_send()

        @when(jnp.logical_and(first, jnp.logical_and(n <= mg, n != mg % BLK)))
        def _(n=n):
            row_copy(n, n).wait_send()

    @when(with_partner)
    def _():
        relay_partner.wait_send()

    for t in range(2):
        tile_col = mb + BLK * t
        wants = jnp.logical_and(tile_col >= 1, mg > tile_col)

        @when(jnp.logical_and(wants, core == tile_col % 2))
        def _(t=t):
            forward(t).wait_send()


def shards(conn, extract, points):
    f32, bf16 = jnp.float32, jnp.bfloat16
    vmem = lambda dtype, *shape: pltpu.VMEM(shape, dtype)
    dma = pltpu.SemaphoreType.DMA
    anywhere = pl.BlockSpec(memory_space=pl.ANY)
    return pl.pallas_call(
        stiffness_kernel,
        out_shape=jax.ShapeDtypeStruct((1, TB, 2, TB), f32),
        in_specs=[anywhere] * 4,
        out_specs=pl.BlockSpec(memory_space=pltpu.VMEM),
        scratch_shapes=[
            vmem(f32, 16, TB),
            vmem(jnp.int32, 16, QP),
            vmem(f32, QP, QP, 16),
            vmem(f32, QP, 3, 16),
            vmem(f32, TB, TB),
            vmem(f32, 2, TB, TB),
            vmem(f32, 2, TB, TB),
            vmem(f32, 18, 16, TB),
            vmem(bf16, 2, WIN, PTS),
            vmem(bf16, 2, WIN, PTS),
            vmem(f32, 2, 16, TB),
            vmem(f32, 2, 4, 16, TB),
            vmem(f32, 3, TB, TB),
            vmem(bf16, PTS, PTS),
            vmem(f32, PTS, WIN),
            vmem(f32, 16, TB),
            vmem(f32, 2, 16, TB),
            vmem(f32, 16, 16, TB),
            vmem(f32, WIN, WIN),
            vmem(f32, 2, TB, TB),
            vmem(f32, 5, 64, TB),
            vmem(f32, 2, 2, TB, TB),
            vmem(f32, 2, 3, 2, 64, TB),
            vmem(f32, 2, TB, TB),
            vmem(f32, TB, TB),
            vmem(f32, TB, TB),
            vmem(f32, 2, TB, TB),
            vmem(f32, TB, WIN),
            dma((4,)),
            dma((8,)),
            dma((9,)),
            dma((2,)),
            dma((16,)),
            dma((7,)),
            dma((2, 2)),
            dma((2, 3, 2)),
            dma((17,)),
            dma((3,)),
            dma((8,)),
            dma,
            dma((11,)),
            dma((2,)),
            pltpu.SemaphoreType.REGULAR,
        ],
        compiler_params=pltpu.CompilerParams(
            collective_id=0, has_side_effects=True, vmem_limit_bytes=VMEM_LIMIT
        ),
        name="stiffness",
    )(jnp.asarray(bernstein_lanes()), conn, extract, points.transpose(1, 0, 2))


def solution(mesh):
    in_specs = (
        P(("blk", "grid"), None),
        P(None, None, ("blk", "grid")),
        P(None, None, ("blk", "grid")),
    )
    out_specs = P(None, "grid", None, "blk")
    return jax.shard_map(shards, mesh=mesh, in_specs=in_specs, out_specs=out_specs, check_vma=False)
```

time: 1190 us -> 55.7 us (0.05)
  blocking collectives: 542 us -> 0 us
  waiting for transfers between devices: 335 us -> 0 us
  local copies, waits for them, and re-layouts: 120 us -> 3.66 us
  other arithmetic: 98.2 us -> 0 us
  matrix products: 70.7 us -> 0 us
  Pallas kernels: 0 us -> 51.2 us
  between operations: 13.4 us -> 0.01 us
    all_gather x3 -> x0, blocking collectives: 542 us -> none  [the longest x1 186 us: shards(): lax.all_gather(points_flat, ('blk', 'grid'), axis=1, tiled=True)]
    unnamed x4 -> x0, waiting for transfers between devices: 216 us -> none
    dot_general x51 -> x0, matrix products: 69.7 us -> none  [the longest x16 38.3 us: step(): jnp.dot(kernel_block, trial_phi, precision=lax.Precision.HIGHEST, preferr...]
    psum x1 -> x0, waiting for transfers between devices: 67 us -> none  [spread(): return lax.psum(jnp.where(mine, array, jnp.zeros_like(array)), axis)]
    all_gather x1 -> x0, waiting for transfers between devices: 51.9 us -> none  [shards(): panel_tiles = lax.all_gather(mine, 'grid', axis=0, tiled=True)]
    pallas_call x0 -> x1, Pallas kernels: none -> 51.2 us  [shards(): pl.pallas_call(stiffness_kernel, out_shape=jax.ShapeDtypeStruct((1, TB, 2...]
    dynamic_update_slice x16 -> x0, local copies, waits for them, and re-layouts: 27.4 us -> none  [step(): lax.dynamic_update_slice_in_dim(potential_wide, current + block, offset, 1)]
    reshape x40 -> x0, local copies, waits for them, and re-layouts: 26.7 us -> none  [the longest x1 18.2 us: shards(): term = placed.reshape(blk_size * grid_size, -1)]
  transfers between devices with their start and end apart: 3 -> 0, of which waited for: 3 -> 0; matrix products, arithmetic and copies ran while one was open for 0% -> 0% of each run, Pallas kernels for 0% -> 0%
where the time goes in v4:
time: 55.7 us; the launch traced here: 54.8 us
  Pallas kernels  51.2 us (92%)
  local copies, waits for them, and re-layouts  3.66 us (7%)
    pallas_call x1, Pallas kernels, shards(): pl.pallas_call(stiffness_kernel, out_shape=jax.ShapeDtypeStruct((1, TB, 2...  51.2 us
    unnamed x9, local copies, waits for them, and re-layouts  3.66 us

profile of v4, /device:TPU:127, one launch (start us, length us, event | category | flops | bytes accessed | tf_op | source)
XLA Modules:
  0.0 54.8 jit_solution(15060748713974996329)
XLA Ops:
  0.0 0.0 copy-start
  0.0 0.9 %copy-done = f32[9,9,16]{2,1,0:T(8,128)S(1)} copy-done((f32[9,9,16]{2,1,0:T(8,128)S(1)}, f32[9,9,16]{2,1,0:T(8,128)}, u32[]{:S(2)}) %copy-start) | copy-done | bytes 5208
  0.9 0.0 copy-start.1
  0.9 0.7 %copy-done.1 = f32[3,9,16]{2,0,1:T(4,128)S(1)} copy-done((f32[3,9,16]{2,0,1:T(4,128)S(1)}, f32[3,9,16]{2,0,1:T(4,128)}, u32[]{:S(2)}) %copy-start.1) | copy-done | bytes 1752
  1.6 0.0 copy-start.2
  1.6 0.7 %copy-done.2 = s32[16,9]{1,0:T(8,128)S(1)} copy-done((s32[16,9]{1,0:T(8,128)S(1)}, s32[16,9]{1,0:T(8,128)}, u32[]{:S(2)}) %copy-start.2) | copy-done | bytes 600
  2.3 0.0 copy-start.3
  2.3 0.7 %copy-done.3 = f32[16,128]{1,0:T(8,128)S(1)} copy-done((f32[16,128]{1,0:T(8,128)S(1)}, f32[16,128]{1,0:T(8,128)}, u32[]{:S(2)}) %copy-start.3) | copy-done | bytes 8216
  3.0 51.2 %stiffness.1 = f32[1,128,2,128]{3,2,1,0:T(2,128)S(1)} custom-call(f32[16,128]{1,0:T(8,128)S(1)} %copy-done.3, s32[16,9]{1,0:T(8,128)S(1)} %copy-done.2, f32[9,9,16]{2,1,0:T(8,128)S(1)} %copy-done, f32[9,3,16]{2,1,0:T(4,128)S(1)} %bitcast.1), custom_call_target="tpu_custom_call" | custom-call | tf_op jit(solution)/shard_map/stiffness/pallas_call | solution.py:749
  54.2 0.7 %copy.6 = f32[1,128,2,128]{3,2,1,0:T(2,128)} copy(f32[1,128,2,128]{3,2,1,0:T(2,128)S(1)} %stiffness.1) | data formatting | bytes 262144
Async XLA Ops:
  0.0 0.9 %copy-start = (f32[9,9,16]{2,1,0:T(8,128)S(1)}, f32[9,9,16]{2,1,0:T(8,128)}, u32[]{:S(2)}) copy-start(f32[9,9,16]{2,1,0:T(8,128)} %extract_in.1) | copy-start | bytes 15556
  0.9 0.7 %copy-start.1 = (f32[3,9,16]{2,0,1:T(4,128)S(1)}, f32[3,9,16]{2,0,1:T(4,128)}, u32[]{:S(2)}) copy-start(f32[3,9,16]{2,0,1:T(4,128)} %param.6) | copy-start | bytes 5188
  1.6 0.7 %copy-start.2 = (s32[16,9]{1,0:T(8,128)S(1)}, s32[16,9]{1,0:T(8,128)}, u32[]{:S(2)}) copy-start(s32[16,9]{1,0:T(8,128)} %conn_in.1) | copy-start | bytes 1732
  2.3 0.7 %copy-start.3 = (f32[16,128]{1,0:T(8,128)S(1)}, f32[16,128]{1,0:T(8,128)}, u32[]{:S(2)}) copy-start(f32[16,128]{1,0:T(8,128)} %constant.2.clone.bern_in) | copy-start | bytes 24580

commit v5 on v4

--- a/solution.py
+++ b/solution.py
@@ -26,7 +26,7 @@
 FX, FY, FW, FV, FC = 0, 9, 18, 27, 108
 
 MESH = pl.DeviceIdType.MESH
-VMEM_LIMIT = 48 * 1024 * 1024
+VMEM_LIMIT = 60 * 1024 * 1024
 EXACT = lax.Precision.HIGHEST
 
 
@@ -135,9 +135,11 @@
     return jnp.concatenate([value, value], axis=1)
 
 
-def eliminate(work):
+def eliminate(work, midway):
     at = lax.broadcasted_iota(jnp.int32, (8, WIN), 0)
     for top in range(0, TB, STEP):
+        if top == TB // 2:
+            midway()
         rows = [jnp.broadcast_to(work[top + i : top + i + 1, :], (8, WIN)) for i in range(STEP)]
         entry = {
             (i, j): jnp.broadcast_to(rows[i][:, top + j : top + j + 1], (8, TB))
@@ -219,8 +221,8 @@
 
 
 def kernel_chunk(i, j, q_slot, trial_x, trial_y, splat, kern):
-    qx = jnp.broadcast_to(trial_x[q_slot, pl.ds(j, 1), :], (8, TB))
-    qy = [jnp.broadcast_to(trial_y[q_slot, quarter, pl.ds(j, 1), :], (8, TB)) for quarter in range(4)]
+    qx = jnp.broadcast_to(trial_x[q_slot, j : j + 1, :], (8, TB))
+    qy = [jnp.broadcast_to(trial_y[q_slot, quarter, j : j + 1, :], (8, TB)) for quarter in range(4)]
     sums = jnp.zeros((8, TB), jnp.float32)
     for h in range(8):
         values = []
@@ -233,9 +235,9 @@
             value = square * square * lax.rsqrt(root)
             sums = sums + value * splat[2, rows, :]
             values.append(value)
-        kern[TB * i + 16 * h : TB * i + 16 * h + 16, pl.ds(pl.multiple_of(j * TB, TB), TB)] = (
-            jnp.concatenate(values, axis=0).astype(jnp.bfloat16)
-        )
+        kern[TB * i + 16 * h : TB * i + 16 * h + 16, TB * j : TB * (j + 1)] = jnp.concatenate(
+            values, axis=0
+        ).astype(jnp.bfloat16)
     return jnp.sum(sums, axis=0, keepdims=True)
 
 
@@ -246,7 +248,7 @@
 def stiffness_kernel(
     bern_in, conn_in, extract_in, points_in, out_ref,
     bern, conn, extract, points, raw, rec, fields, spread, phi_hi, phi_lo, trial_x, trial_y, splat, kern, pot,
-    col_sum, totals, parts, xs, stage_big, stage_small, land_big, land_small, tiles, head, row_tile, col_tile, work,
+    col_sum, totals, parts, xs, own_x, stage_big, stage_small, land_big, land_small, tiles, head, row_tile, col_tile, work,
     in_sem, rec_send, rec_recv, total_send, total_recv, piece_send, big_recv, small_recv,
     head_send, head_recv, row_send, row_recv, col_send, col_recv, ready,
 ):
@@ -302,85 +304,101 @@
     block_copy.start()
 
     other = (own + 1 + place) % 16
-    set_up_block(0, own, -HALF_X, rec, fields, spread, phi_hi, phi_lo, trial_x, trial_y)
-    block_copy.wait_recv()
-    wrapped = jnp.where(other < own, HALF_X, -HALF_X)
-    set_up_block(1, other, wrapped, rec, fields, spread, phi_hi, phi_lo, trial_x, trial_y)
-
     lower = own < 8
 
-    def evaluate(i, low, high, q_slot):
-        def part(j, carry):
-            col_sum[pl.ds(j, 1), :] += kernel_chunk(i, j, q_slot, trial_x, trial_y, splat, kern)
-            return carry
-
-        steps = high - low
-        lax.fori_loop(low, high, part, 0, unroll=3 if steps % 3 == 0 else 2 if steps % 2 == 0 else 1)
-
-    def run(r):
-        q_slot = 1 - r
-        col_sum[...] = jnp.zeros_like(col_sum)
-        if r == 0:
-            @when(jnp.logical_and(last, lower))
-            def _():
-                kern[5 * TB : PTS, :] = jnp.zeros((4 * TB, PTS), jnp.bfloat16)
-
-            @when(jnp.logical_and(last, jnp.logical_not(lower)))
-            def _():
-                kern[:, 0 : 5 * TB] = jnp.zeros((PTS, 5 * TB), jnp.bfloat16)
-
-        for i in range(QP):
-            for n, field in ((0, FX), (1, FY), (2, FW)):
-                picked = rec[0, :, field + i : field + i + 1] * (EX / 2.0 if n < 2 else KERNEL_GAIN)
-                splat[n] = jnp.broadcast_to(picked, (TB, TB))
-            if r == 1:
-                at = slice(TB * i, TB * (i + 1))
-                if i > 0:
-                    kern[at, 0 : TB * i] = jnp.zeros((TB, TB * i), jnp.bfloat16)
-                col_sum[i : i + 1, :] += 0.5 * kernel_chunk(i, i, q_slot, trial_x, trial_y, splat, kern)
-                kern[at, at] = kern[at, at] * 0.5
-                if i + 1 < QP:
-                    evaluate(i, i + 1, QP, q_slot)
-                continue
-            whole = jnp.logical_not(last)
-            if i < 5:
-                whole = jnp.logical_or(whole, lower)
-
-            @when(whole)
-            def _(i=i):
-                evaluate(i, 0, QP, q_slot)
-
-            @when(jnp.logical_and(last, jnp.logical_not(lower)))
-            def _(i=i):
-                evaluate(i, 5, QP, q_slot)
-
-        pot[...] = nt(kern[...], phi_hi[q_slot]) + nt(kern[...], phi_lo[q_slot])
-
-        columns = [
-            pot[TB * i : TB * (i + 1), TB:WIN].T[AUG - TB : AUG - TB + 1, :] * KERNEL_GAIN for i in range(QP)
-        ]
-        if r == 0:
-            totals[1, 0:QP, :] = col_sum[0:QP, :]
-            for i in range(QP):
-                totals[0, i : i + 1, :] = columns[i]
-            total_copy(1).start()
-
-            @when(jnp.logical_not(last))
-            def _():
-                total_copy(0).start()
-        else:
-            for i in range(QP):
-                parts[7, i : i + 1, :] = totals[0, i : i + 1, :] + col_sum[i : i + 1, :] + columns[i]
-
+    def test_points(i):
+        for n, field in ((0, FX), (1, FY), (2, FW)):
+            picked = rec[0, :, field + i : field + i + 1] * (EX / 2.0 if n < 2 else KERNEL_GAIN)
+            splat[n] = jnp.broadcast_to(picked, (TB, TB))
+
+    def evaluate(i, columns, q_slot):
+        for j in columns:
+            col_sum[j : j + 1, :] += kernel_chunk(i, j, q_slot, trial_x, trial_y, splat, kern)
+
+    def multiply(rows, points, q_slot):
+        pot[rows, :] = nt(kern[rows, points], phi_hi[q_slot, :, points]) + nt(
+            kern[rows, points], phi_lo[q_slot, :, points]
+        )
+
+    def row_sums():
+        return [pot[TB * i : TB * (i + 1), TB:WIN].T[AUG - TB : AUG - TB + 1, :] * KERNEL_GAIN for i in range(QP)]
+
+    def window():
         high, low = split(pot[...])
         inside = jnp.logical_and(
             lax.broadcasted_iota(jnp.int32, (WIN, WIN), 0) < AUG,
             lax.broadcasted_iota(jnp.int32, (WIN, WIN), 1) < AUG,
         )
         value = nn(phi_hi[0], high) + nn(phi_lo[0], high) + nn(phi_hi[0], low)
-        xs[...] = jnp.where(inside, -KERNEL_GAIN * value, 0.0)
-        if r == 0:
-            pair_pieces()
+        return jnp.where(inside, -KERNEL_GAIN * value, 0.0)
+
+    every = slice(0, PTS)
+    split_at = 5 * TB
+
+    def run_diagonal():
+        middle = 4 * TB
+        col_sum[...] = jnp.zeros_like(col_sum)
+        for i in range(QP):
+            test_points(i)
+            at = slice(TB * i, TB * (i + 1))
+            start = 0 if i < 4 else middle
+            if TB * i > start:
+                kern[at, start : TB * i] = jnp.zeros((TB, TB * i - start), jnp.bfloat16)
+            col_sum[i : i + 1, :] += 0.5 * kernel_chunk(i, i, 0, trial_x, trial_y, splat, kern)
+            kern[at, at] = kern[at, at] * 0.5
+            evaluate(i, range(i + 1, QP), 0)
+        multiply(slice(0, middle), every, 0)
+        multiply(slice(middle, PTS), slice(middle, PTS), 0)
+        for i, value in enumerate(row_sums()):
+            parts[7, i : i + 1, :] = col_sum[i : i + 1, :] + value
+        own_x[...] = window()
+
+    def run_pair():
+        low_last = jnp.logical_and(last, lower)
+        high_last = jnp.logical_and(last, jnp.logical_not(lower))
+        col_sum[...] = jnp.zeros_like(col_sum)
+        for i in range(QP):
+            test_points(i)
+            whole = jnp.logical_not(last)
+            if TB * i < split_at:
+                whole = jnp.logical_or(whole, lower)
+
+            @when(whole)
+            def _(i=i):
+                evaluate(i, range(QP), 1)
+
+            @when(high_last)
+            def _(i=i):
+                evaluate(i, range(5, QP), 1)
+
+        @when(jnp.logical_not(last))
+        def _():
+            multiply(every, every, 1)
+
+        @when(low_last)
+        def _():
+            multiply(slice(0, split_at), every, 1)
+            pot[split_at:PTS, :] = jnp.zeros((PTS - split_at, WIN), jnp.float32)
+
+        @when(high_last)
+        def _():
+            multiply(every, slice(split_at, PTS), 1)
+
+        totals[1, 0:QP, :] = col_sum[0:QP, :]
+        total_copy(1).start()
+        for i, value in enumerate(row_sums()):
+            totals[0, i : i + 1, :] = value
+
+        @when(jnp.logical_not(last))
+        def _():
+            total_copy(0).start()
+
+        @when(last)
+        def _():
+            parts[7, 0:QP, :] += totals[0, 0:QP, :]
+
+        xs[...] = window()
+        pair_pieces()
 
     def total_copy(n):
         b, g = column_device(other if n == 1 else own, 7)
@@ -463,11 +481,19 @@
 
         send_piece(3)
 
-    run(0)
-
+    set_up_block(0, own, -HALF_X, rec, fields, spread, phi_hi, phi_lo, trial_x, trial_y)
     @when(last)
     def _():
-        run(1)
+        run_diagonal()
+
+    block_copy.wait_recv()
+    wrapped = jnp.where(other < own, HALF_X, -HALF_X)
+    set_up_block(1, other, wrapped, rec, fields, spread, phi_hi, phi_lo, trial_x, trial_y)
+
+    run_pair()
+
+    @when(last)
+    def _():
         build_phi(fields.at[0], own * TB, False, spread, phi_hi.at[1], phi_lo.at[1])
         for ref in (phi_hi, phi_lo):
             ref[1, AUG:WIN, :] = jnp.zeros((WIN - AUG, PTS), jnp.bfloat16)
@@ -477,7 +503,7 @@
         gain = parts[0]
         for n in range(1, 16):
             gain = gain + parts[n]
-        mass = xs[...] + xs[...].T
+        mass = own_x[...] + own_x[...].T
         for k in range(QP):
             lanes = slice(TB * k, TB * (k + 1))
             left = phi_hi[1, :, lanes].astype(jnp.float32) + phi_lo[1, :, lanes].astype(jnp.float32)
@@ -551,8 +577,18 @@
     relay = jnp.logical_and(mg >= 1, mb == mg % BLK)
     special = jnp.logical_and(first, mg % BLK != 0)
 
-    def row_copy(n, b):
-        return remote(tiles.at[0], row_tile, row_send.at[n], row_recv, b, mg)
+    def row_copy(n, b, src=None):
+        return remote(tiles.at[0] if src is None else src, row_tile, row_send.at[n], row_recv, b, mg)
+
+    edges = [(0, 4, 1, None), (0, 1, 2, None), (0, 3, 3, None), (4, 5, 1, None), (4, 7, 2, None)]
+    edges += [(1, 2, 1, 0), (3, 2, 1, 1), (5, 6, 1, 0), (7, 6, 1, 1)]
+
+    def edge_on(parent, child, which):
+        on = jnp.logical_and(mb == parent, jnp.logical_and(mg >= child, mg % BLK != child))
+        return on if which is None else jnp.logical_and(on, core == which)
+
+    def edge_copy(parent, child, n):
+        return row_copy(n, child, None if parent == 0 else row_tile)
 
     @when(special)
     def _():
@@ -581,6 +617,11 @@
     def _():
         for n in range(1, 8):
             head_half(n, 0, 2 * n + core, half_rows).start()
+
+    for parent, child, n, which in edges[:3]:
+        @when(edge_on(parent, child, which))
+        def _(parent=parent, child=child, n=n):
+            edge_copy(parent, child, n).start()
 
     @when(jnp.logical_and(first, mg == 8))
     def _():
@@ -594,9 +635,19 @@
     )
     with_partner = jnp.logical_and(relay, core == 0)
 
-    @when(jnp.logical_and(relay, jnp.logical_not(first)))
+    early = relay
+    for parent, child, n, which in edges[3:]:
+        early = jnp.logical_or(early, edge_on(parent, child, which))
+    early = jnp.logical_and(early, jnp.logical_not(first))
+
+    @when(early)
     def _():
         row_copy(0, mb).wait_recv()
+
+    for parent, child, n, which in edges[3:]:
+        @when(edge_on(parent, child, which))
+        def _(parent=parent, child=child, n=n):
+            edge_copy(parent, child, n).start()
 
     for n in range(1, 8):
         @when(jnp.logical_and(relay, chip < n))
@@ -622,11 +673,6 @@
     def _():
         head_swap(half_rows, partner).start()
 
-    for n in range(1, 8):
-        @when(jnp.logical_and(first, jnp.logical_and(n <= mg, n != mg % BLK)))
-        def _(n=n):
-            row_copy(n, n).start()
-
     @when(swaps)
     def _():
         head_swap(other_rows, partner).wait_recv()
@@ -634,19 +680,20 @@
     def forward(t):
         return remote(col_tile.at[t], col_tile.at[t], col_send.at[9 + t], col_recv.at[t], mb, partner)
 
-    for t in range(2):
-        tile_col = mb + BLK * t
-        wants = jnp.logical_and(tile_col >= 1, mg > tile_col)
-
-        @when(wants)
-        def _(t=t, tile_col=tile_col):
-            forward(t).wait_recv()
-
-            @when(core == tile_col % 2)
-            def _():
-                forward(t).start()
-
-    needs_row = jnp.logical_and(jnp.logical_not(first), jnp.logical_and(mb <= mg, jnp.logical_not(relay)))
+    def columns_in():
+        for t in range(2):
+            tile_col = mb + BLK * t
+            wants = jnp.logical_and(tile_col >= 1, mg > tile_col)
+
+            @when(wants)
+            def _(t=t, tile_col=tile_col):
+                forward(t).wait_recv()
+
+                @when(core == tile_col % 2)
+                def _():
+                    forward(t).start()
+
+    needs_row = jnp.logical_and(jnp.logical_not(first), jnp.logical_and(mb <= mg, jnp.logical_not(early)))
 
     row = lax.broadcasted_iota(jnp.int32, (TB, TB), 0)
     col = lax.broadcasted_iota(jnp.int32, (TB, TB), 1)
@@ -656,7 +703,7 @@
     def _():
         work[:, 0:TB] = 0.5 * (head[...] + head[...].T)
         work[:, TB:WIN] = jnp.where(row == col, 1.0, 0.0)
-        eliminate(work)
+        eliminate(work, columns_in)
 
         @when(needs_row)
         def _():
@@ -724,9 +771,11 @@
         def _(n=n):
             head_half(7 + n, n, mg, half_rows).wait_send()
 
-        @when(jnp.logical_and(first, jnp.logical_and(n <= mg, n != mg % BLK)))
-        def _(n=n):
-            row_copy(n, n).wait_send()
+
+    for parent, child, n, which in edges:
+        @when(edge_on(parent, child, which))
+        def _(parent=parent, child=child, n=n):
+            edge_copy(parent, child, n).wait_send()
 
     @when(with_partner)
     def _():
@@ -745,7 +794,7 @@
     f32, bf16 = jnp.float32, jnp.bfloat16
     vmem = lambda dtype, *shape: pltpu.VMEM(shape, dtype)
     dma = pltpu.SemaphoreType.DMA
-    anywhere = pl.BlockSpec(memory_space=pl.ANY)
+    anywhere = pl.BlockSpec(memory_space=pltpu.HBM)
     return pl.pallas_call(
         stiffness_kernel,
         out_shape=jax.ShapeDtypeStruct((1, TB, 2, TB), f32),
@@ -770,6 +819,7 @@
             vmem(f32, 16, TB),
             vmem(f32, 2, 16, TB),
             vmem(f32, 16, 16, TB),
+            vmem(f32, WIN, WIN),
             vmem(f32, WIN, WIN),
             vmem(f32, 2, TB, TB),
             vmem(f32, 5, 64, TB),

time: 55.7 us -> 52.1 us (0.935)
  local copies, waits for them, and re-layouts: 3.66 us -> 1.57 us
  Pallas kernels: 51.2 us -> 49.7 us
    unnamed x9 -> x1, local copies, waits for them, and re-layouts: 3.66 us -> 1.57 us
    pallas_call x1, Pallas kernels: 51.2 us -> 49.7 us  [shards(): pl.pallas_call(stiffness_kernel, out_shape=jax.ShapeDtypeStruct((1, TB, 2...]
where the time goes in v5:
time: 52.1 us; the launch traced here: 51.3 us
  Pallas kernels  49.7 us (95%)
  local copies, waits for them, and re-layouts  1.57 us (3%)
    pallas_call x1, Pallas kernels, shards(): pl.pallas_call(stiffness_kernel, out_shape=jax.ShapeDtypeStruct((1, TB, 2...  49.7 us
    unnamed x1, local copies, waits for them, and re-layouts  1.57 us

profile of v5, /device:TPU:127, one launch (start us, length us, event | category | flops | bytes accessed | tf_op | source)
XLA Modules:
  0.0 51.3 jit_solution(16679787888474125506)
XLA Ops:
  0.0 49.7 %stiffness.1 = f32[1,128,2,128]{3,2,1,0:T(2,128)} custom-call(f32[16,128]{1,0:T(8,128)} %constant.2.clone.bern_in, s32[16,9]{1,0:T(8,128)} %conn_in.1, f32[9,9,16]{2,1,0:T(8,128)} %extract_in.1, f32[9,3,16]{2,1,0:T(4,128)} %bitcast.1), custom_call_target="tpu_custom_call" | custom-call | tf_op jit(solution)/shard_map/stiffness/pallas_call | solution.py:798
  49.7 1.6 %copy.6 = f32[1,128,2,128]{3,2,1,0:T(2,128)} copy(f32[1,128,2,128]{3,2,1,0:T(2,128)} %stiffness.1) | data formatting | bytes 262144

commit v6 on v5

--- a/solution.py
+++ b/solution.py
@@ -321,7 +321,10 @@
         )
 
     def row_sums():
-        return [pot[TB * i : TB * (i + 1), TB:WIN].T[AUG - TB : AUG - TB + 1, :] * KERNEL_GAIN for i in range(QP)]
+        pick = (lax.broadcasted_iota(jnp.int32, (16, TB), 1) == AUG - TB).astype(jnp.bfloat16)
+        high, low = split(pot[:, TB:WIN])
+        sums = (nt(pick, high) + nt(pick, low)) * KERNEL_GAIN
+        return [sums[0:1, TB * i : TB * (i + 1)] for i in range(QP)]
 
     def window():
         high, low = split(pot[...])
@@ -525,7 +528,7 @@
         for n in range(4, 7):
             settle_piece(n)
 
-    for t in range(2):
+    def sum_tile(t):
         tile_col = mb + BLK * t
         owned = mg >= tile_col
         square = mg == tile_col
@@ -570,7 +573,11 @@
                             tiles[t] += below(dst[...]).T
 
     first = mb == 0
-    upper_half = core == 0
+
+    @when(first)
+    def _():
+        sum_tile(0)
+
     half_rows = pl.ds(pl.multiple_of(64 * core, 64), 64)
     other_rows = pl.ds(pl.multiple_of(64 * (1 - core), 64), 64)
     active = mb <= 2 * chip + 1
@@ -633,7 +640,12 @@
     relay_partner = remote(
         row_tile, col_tile.at[mg // BLK], col_send.at[8], col_recv.at[mg // BLK], mb, partner
     )
-    with_partner = jnp.logical_and(relay, core == 0)
+    helper = jnp.logical_and(partner >= 1, mb == partner % BLK)
+
+    def helper_copy(n):
+        view = col_tile.at[mg // BLK]
+        return remote(view, view, col_send.at[n], col_recv.at[mg // BLK], mb, 2 * n + core)
+
 
     early = relay
     for parent, child, n, which in edges[3:]:
@@ -649,14 +661,23 @@
         def _(parent=parent, child=child, n=n):
             edge_copy(parent, child, n).start()
 
-    for n in range(1, 8):
+    @when(relay)
+    def _():
+        relay_partner.start()
+
+    for n in (2, 4, 6):
         @when(jnp.logical_and(relay, chip < n))
         def _(n=n):
             relay_copy(n).start()
 
-    @when(with_partner)
-    def _():
-        relay_partner.start()
+    @when(helper)
+    def _():
+        helper_copy(0).wait_recv()
+
+    for n in (1, 3, 5, 7):
+        @when(jnp.logical_and(helper, chip < n))
+        def _(n=n):
+            helper_copy(n).start()
 
     @when(jnp.logical_and(active, jnp.logical_not(root_pair)))
     def _():
@@ -683,13 +704,13 @@
     def columns_in():
         for t in range(2):
             tile_col = mb + BLK * t
-            wants = jnp.logical_and(tile_col >= 1, mg > tile_col)
+            wants = jnp.logical_and(tile_col >= 1, chip > tile_col // 2)
 
             @when(wants)
             def _(t=t, tile_col=tile_col):
                 forward(t).wait_recv()
 
-                @when(core == tile_col % 2)
+                @when(core == (tile_col + chip) % 2)
                 def _():
                     forward(t).start()
 
@@ -704,6 +725,13 @@
         work[:, 0:TB] = 0.5 * (head[...] + head[...].T)
         work[:, TB:WIN] = jnp.where(row == col, 1.0, 0.0)
         eliminate(work, columns_in)
+
+        @when(jnp.logical_not(first))
+        def _():
+            sum_tile(0)
+
+        sum_tile(1)
+
 
         @when(needs_row)
         def _():
@@ -763,9 +791,9 @@
         head_swap(half_rows, partner).wait_send()
 
     for n in range(1, 8):
-        @when(jnp.logical_and(relay, chip < n))
+        @when(jnp.logical_and(relay if n % 2 == 0 else helper, chip < n))
         def _(n=n):
-            relay_copy(n).wait_send()
+            (relay_copy(n) if n % 2 == 0 else helper_copy(n)).wait_send()
 
         @when(jnp.logical_and(first, n <= 2 * chip + 1))
         def _(n=n):
@@ -777,15 +805,15 @@
         def _(parent=parent, child=child, n=n):
             edge_copy(parent, child, n).wait_send()
 
-    @when(with_partner)
+    @when(relay)
     def _():
         relay_partner.wait_send()
 
     for t in range(2):
         tile_col = mb + BLK * t
-        wants = jnp.logical_and(tile_col >= 1, mg > tile_col)
-
-        @when(jnp.logical_and(wants, core == tile_col % 2))
+        wants = jnp.logical_and(tile_col >= 1, chip > tile_col // 2)
+
+        @when(jnp.logical_and(wants, core == (tile_col + chip) % 2))
         def _(t=t):
             forward(t).wait_send()
 

time: 52.1 us -> 52.4 us (level); the launches traced: 51.3 us -> 52.2 us
  Pallas kernels: 49.7 us -> 50.6 us
    pallas_call x1, Pallas kernels: 49.7 us -> 50.6 us  [shards(): pl.pallas_call(stiffness_kernel, out_shape=jax.ShapeDtypeStruct((1, TB, 2...]
where the time goes in v6:
time: 52.4 us; the launch traced here: 52.2 us
  Pallas kernels  50.6 us (97%)
  local copies, waits for them, and re-layouts  1.57 us (3%)
    pallas_call x1, Pallas kernels, shards(): pl.pallas_call(stiffness_kernel, out_shape=jax.ShapeDtypeStruct((1, TB, 2...  50.6 us
    unnamed x1, local copies, waits for them, and re-layouts  1.57 us

profile of v6, /device:TPU:127, one launch (start us, length us, event | category | flops | bytes accessed | tf_op | source)
XLA Modules:
  0.0 52.2 jit_solution(5210793438937875844)
XLA Ops:
  0.0 50.6 %stiffness.1 = f32[1,128,2,128]{3,2,1,0:T(2,128)} custom-call(f32[16,128]{1,0:T(8,128)} %constant.2.clone.bern_in, s32[16,9]{1,0:T(8,128)} %conn_in.1, f32[9,9,16]{2,1,0:T(8,128)} %extract_in.1, f32[9,3,16]{2,1,0:T(4,128)} %bitcast.1), custom_call_target="tpu_custom_call" | custom-call | tf_op jit(solution)/shard_map/stiffness/pallas_call | solution.py:826
  50.6 1.6 %copy.6 = f32[1,128,2,128]{3,2,1,0:T(2,128)} copy(f32[1,128,2,128]{3,2,1,0:T(2,128)} %stiffness.1) | data formatting | bytes 262144
